TPU v7x, 128 devices: a whole 4x4x4 slice. The times are simulated.
128 devices in a mesh: row: 8 (over y, core), col: 16 (over z, x).
Axes of the slice: x: 4, y: 4, z: 4, core: 2. Of those that a mesh axis runs over, the one named last changes fastest.
Arguments:
- child_fronts: float32 [2, 8192, 8192], P(None, 'row', 'col'), as said below
- parent_front: float32 [12288, 12288], P('row', 'col'), as said below
- child_map: int32 [2, 7168], replicated, may hold values from 0 to 12287, as said below
Outputs:
- child_factor: float32 [2, 8192, 1024], P(None, 'row', 'col')
- parent_factor: float32 [12288, 256], P('row', 'col')
- parent_schur: float32 [12288, 12288], P('row', 'col')
Inputs may be any that keep to these rules, and one draw needn't show every extreme that they name: child_fronts[k] and parent_front are symmetric positive definite. parent_front is symmetric positive definite. The entries of child_map[k] are distinct. Each aligned block of 512 entries of child_map[k] names exactly 32 indices in each aligned block of 768 parent indices.
All inputs are finite; a program needn't handle non-finite values.
Results may differ from a plain program's by a relative error of at most 0.0003.
Values sent between devices are 32-bit elements; how exact they have to be, the bound alone decides.
No kernel may reach another device: no remote copies, remote signals or barrier semaphores. Data moves between devices by JAX's collectives and lax.ppermute only.
A program may use at most 192 MiB of HBM per device.

v0:
```python
from functools import partial

import jax
import jax.numpy as jnp
from jax import lax
from jax.sharding import PartitionSpec as P

PP = 256
NB = 256


exact_mode = lax.Precision.HIGHEST


def from_root(value, axis, source):
    kept = jnp.where(lax.axis_index(axis) == source, value, 0).astype(value.dtype)
    return lax.psum(kept, axis)


def outer_update(factor_rows, crossed):
    return jnp.einsum("kin,kjn->kij", factor_rows, crossed, precision=exact_mode)


def take_rows(block, order):
    return jax.vmap(lambda single, picks: jnp.take(single, picks, axis=0))(block, order)


def take_both(block, row_order, col_order):
    rows_first = take_rows(block, row_order)
    flipped = take_rows(jnp.swapaxes(rows_first, 1, 2), col_order)
    return jnp.swapaxes(flipped, 1, 2)


def eliminate(tiles, pivots, send_panel, send_corner, send_cross):
    members, tile_rows, tile_cols = tiles.shape
    row_index = lax.axis_index("row")
    col_index = lax.axis_index("col")
    global_rows = row_index * tile_rows + jnp.arange(tile_rows, dtype=jnp.int32)
    total_steps = pivots // NB
    identity = jnp.broadcast_to(jnp.eye(NB, dtype=jnp.float32), (members, NB, NB))
    collected = []
    current = send_panel(lax.slice_in_dim(tiles, 0, NB, axis=2), 0)
    for panel_step in range(total_steps):
        offset = panel_step * NB
        owner_row = offset // tile_rows
        within_row = offset - owner_row * tile_rows
        corner = send_corner(
            lax.slice_in_dim(current, within_row, within_row + NB, axis=1), owner_row
        )
        factor = jnp.linalg.cholesky(corner)
        inverse = jax.vmap(partial(jax.scipy.linalg.solve_triangular, lower=True))(factor, identity)
        solved = jnp.einsum("krn,kmn->krm", current, inverse, precision=exact_mode)
        factor_rows = jnp.where((global_rows >= offset)[None, :, None], solved, jnp.float32(0.0))
        cross_first = col_index * tile_cols
        cross_owner = cross_first // tile_rows
        local_first = jnp.clip(cross_first - row_index * tile_rows, 0, tile_rows - tile_cols)
        crossed = send_cross(
            lax.dynamic_slice_in_dim(factor_rows, local_first, tile_cols, axis=1), cross_owner
        )
        collected.append(factor_rows)
        if panel_step + 1 < total_steps:
            upcoming = offset + NB
            next_owner = upcoming // tile_cols
            next_within = upcoming - next_owner * tile_cols
            tiles = tiles - outer_update(factor_rows, crossed)
            current = send_panel(
                lax.slice_in_dim(tiles, next_within, next_within + NB, axis=2), next_owner
            )
        else:
            tiles = tiles - outer_update(factor_rows, crossed)
    return (tiles, jnp.concatenate(collected, axis=2))


def inverse_list(targets, length, filler):
    sources = jnp.arange(targets.shape[0], dtype=jnp.int32)
    start = jnp.full((length,), filler, jnp.int32)
    return start.at[targets].set(sources, mode="drop")


def extend_add(tiles, child_map, parent_front):
    members, tile_rows, tile_cols = tiles.shape
    row_count = lax.axis_size("row")
    col_count = lax.axis_size("col")
    row_index = lax.axis_index("row")
    col_index = lax.axis_index("col")
    width = tile_rows * row_count
    pivots = width - child_map.shape[1]
    parent_rows = parent_front.shape[0]
    parent_cols = parent_front.shape[1]
    row_slots = tile_rows // row_count
    col_slots = tile_cols // col_count
    full_map = jnp.concatenate([jnp.zeros((members, pivots), jnp.int32), child_map], axis=1)
    positions = jnp.arange(width, dtype=jnp.int32)[None, :]
    row_keys = jnp.where(positions < pivots, row_count, full_map // parent_rows)
    col_keys = jnp.where(positions < pivots, col_count, full_map // parent_cols)
    row_orders = jnp.argsort(row_keys.reshape(members, row_count, tile_rows), axis=2, stable=True)
    col_orders = jnp.argsort(col_keys.reshape(members, col_count, tile_cols), axis=2, stable=True)
    row_blocks = jnp.arange(row_count, dtype=jnp.int32)
    col_blocks = jnp.arange(col_count, dtype=jnp.int32)
    row_live = jnp.clip((row_blocks + 1) * tile_rows - pivots, 0, tile_rows) // row_count
    col_live = jnp.clip((col_blocks + 1) * tile_cols - pivots, 0, tile_cols) // col_count
    row_seats = jnp.arange(row_slots, dtype=jnp.int32)
    col_seats = jnp.arange(col_slots, dtype=jnp.int32)
    own_row_live = row_live[row_index]
    send_row_pos = jnp.minimum(
        row_blocks[:, None] * own_row_live + row_seats[None, :], tile_rows - 1
    )
    send_row_keep = jnp.broadcast_to(
        row_seats[None, :] < own_row_live, (row_count, row_slots)
    ).reshape(-1)
    own_row_order = jnp.take(row_orders, row_index, axis=1)
    send_rows = jnp.take(own_row_order, send_row_pos.reshape(-1), axis=1)
    own_col_live = col_live[col_index]
    send_col_pos = jnp.minimum(
        col_blocks[:, None] * own_col_live + col_seats[None, :], tile_cols - 1
    )
    send_col_keep = jnp.broadcast_to(
        col_seats[None, :] < own_col_live, (col_count, col_slots)
    ).reshape(-1)
    own_col_order = jnp.take(col_orders, col_index, axis=1)
    send_cols = jnp.take(own_col_order, send_col_pos.reshape(-1), axis=1)
    picked = take_both(tiles, send_rows, send_cols)
    picked = jnp.where(
        send_row_keep[None, :, None] & send_col_keep[None, None, :], picked, jnp.float32(0.0)
    )
    outgoing = jnp.transpose(
        picked.reshape(members, row_count, row_slots, col_count, col_slots), (1, 3, 0, 2, 4)
    )
    flat = outgoing.reshape(row_count * col_count, members, row_slots, col_slots)
    arrived = lax.all_to_all(flat, ("row", "col"), split_axis=0, concat_axis=0, tiled=True)
    arrived = arrived.reshape(row_count, col_count, members, row_slots, col_slots)
    received = jnp.transpose(arrived, (2, 0, 3, 1, 4)).reshape(members, tile_rows, tile_cols)
    recv_row_pos = jnp.minimum(row_index * row_live[:, None] + row_seats[None, :], tile_rows - 1)
    recv_row_keep = (row_seats[None, :] < row_live[:, None]).reshape(-1)
    local_rows = jnp.take_along_axis(row_orders, recv_row_pos[None, :, :], axis=2)
    global_rows = (row_blocks[None, :, None] * tile_rows + local_rows).reshape(members, -1)
    target_rows = jnp.take_along_axis(full_map, global_rows, axis=1) - row_index * parent_rows
    target_rows = jnp.where(recv_row_keep[None, :], target_rows, parent_rows)
    recv_col_pos = jnp.minimum(col_index * col_live[:, None] + col_seats[None, :], tile_cols - 1)
    recv_col_keep = (col_seats[None, :] < col_live[:, None]).reshape(-1)
    local_cols = jnp.take_along_axis(col_orders, recv_col_pos[None, :, :], axis=2)
    global_cols = (col_blocks[None, :, None] * tile_cols + local_cols).reshape(members, -1)
    target_cols = jnp.take_along_axis(full_map, global_cols, axis=1) - col_index * parent_cols
    target_cols = jnp.where(recv_col_keep[None, :], target_cols, parent_cols)
    row_sources = jax.vmap(lambda targets: inverse_list(targets, parent_rows, tile_rows))(
        target_rows
    )
    col_sources = jax.vmap(lambda targets: inverse_list(targets, parent_cols, tile_cols))(
        target_cols
    )
    padded = jnp.concatenate([received, jnp.zeros((members, 1, tile_cols), jnp.float32)], axis=1)
    placed_rows = take_rows(padded, row_sources)
    flipped = jnp.swapaxes(placed_rows, 1, 2)
    flipped = jnp.concatenate([flipped, jnp.zeros((members, 1, parent_rows), jnp.float32)], axis=1)
    placed = jnp.swapaxes(take_rows(flipped, col_sources), 1, 2)
    merged = parent_front
    for which_child in range(members):
        merged = merged + placed[which_child]
    return merged


def child_panel(piece, owner):
    return from_root(piece, "col", owner)


def child_corner(piece, owner):
    return from_root(piece, "row", owner)


def child_cross(piece, owner):
    return from_root(piece, "row", owner)


def parent_panel(piece, owner):
    return from_root(piece, "col", owner)


def parent_corner(piece, owner):
    return from_root(piece, "row", owner)


def parent_cross(piece, owner):
    return from_root(piece, "row", owner)


def local(child_fronts, parent_front, child_map):
    col_count = lax.axis_size("col")
    row_index = lax.axis_index("row")
    col_index = lax.axis_index("col")
    tile_rows = child_fronts.shape[1]
    width = tile_rows * lax.axis_size("row")
    pivots = width - child_map.shape[1]
    updated, child_panels = eliminate(child_fronts, pivots, child_panel, child_corner, child_cross)
    merged = extend_add(updated, child_map, parent_front)
    parent_updated, parent_panels = eliminate(
        merged[None], PP, parent_panel, parent_corner, parent_cross
    )
    child_share = pivots // col_count
    child_factor = lax.dynamic_slice_in_dim(
        child_panels, col_index * child_share, child_share, axis=2
    )
    parent_share = PP // col_count
    parent_factor = lax.dynamic_slice_in_dim(
        parent_panels[0], col_index * parent_share, parent_share, axis=1
    )
    parent_rows = parent_front.shape[0]
    parent_cols = parent_front.shape[1]
    global_rows = row_index * parent_rows + jnp.arange(parent_rows, dtype=jnp.int32)
    global_cols = col_index * parent_cols + jnp.arange(parent_cols, dtype=jnp.int32)
    keep = (global_rows[:, None] >= PP) & (global_cols[None, :] >= PP)
    parent_schur = jnp.where(keep, parent_updated[0], jnp.float32(0.0))
    return (child_factor, parent_factor, parent_schur)


def solution(mesh):
    placed = (P(None, "row", "col"), P("row", "col"), P())
    return jax.shard_map(
        local,
        mesh=mesh,
        in_specs=placed,
        out_specs=(P(None, "row", "col"), P("row", "col"), P("row", "col")),
        check_vma=False,
    )
```

profile of v0, /device:TPU:0, one launch (start us, length us, event | category | flops | bytes accessed | tf_op | source)
XLA Modules:
  0.0 2048.4 jit_solution(9405431235240546591)
XLA Ops:
  16.8 92.8 %all-reduce.21.cloned.1.call-done = f32[2,1024,256]{1,2,0:T(8,128)} async-done(((f32[2,1024,256]{1,2,0:T(8,128)}), f32[2,1024,256]{1,2,0:T(8,128)}) %all-reduce.21.cloned.1.call-update) | async-done | bytes 2097168 | tf_op jit(solution)/shard_map/psum | solution.py:17
  111.5 61.1 %all-reduce.23.cloned.1.call-done = f32[2,256,256]{1,2,0:T(8,128)} async-done(((f32[2,256,256]{1,2,0:T(8,128)}), f32[2,256,256]{1,2,0:T(8,128)}) %all-reduce.23.cloned.1.call-update) | async-done | bytes 524304 | tf_op jit(solution)/shard_map/psum | solution.py:17
  246.8 39.5 %custom-call.65 = f32[2,2,128,128]{2,3,1,0:T(8,128)S(1)} custom-call(f32[2,2,128,128]{3,2,1,0:T(8,128)S(1)} %bitcast.389), custom_call_target="InvertDiagBlocksLowerTriangular" | custom-call | tf_op jit(solution)/shard_map/vmap(jit(_solve_triangular))/triangular_solve | solution.py:51
  292.8 61.7 %all-reduce.25.cloned.1.call-done = f32[2,512,256]{1,2,0:T(8,128)} async-done(((f32[2,512,256]{1,2,0:T(8,128)}), f32[2,512,256]{1,2,0:T(8,128)}) %all-reduce.25.cloned.1.call-update) | async-done | bytes 1048592 | tf_op jit(solution)/shard_map/psum | solution.py:17
  365.3 89.7 %all-reduce.27.cloned.1.call-done = f32[2,1024,256]{1,2,0:T(8,128)} async-done(((f32[2,1024,256]{1,2,0:T(8,128)}), f32[2,1024,256]{1,2,0:T(8,128)}) %all-reduce.27.cloned.1.call-update) | async-done | bytes 2097168 | tf_op jit(solution)/shard_map/psum | solution.py:17
  457.0 61.0 %all-reduce.29.cloned.1.call-done = f32[2,256,256]{1,2,0:T(8,128)} async-done(((f32[2,256,256]{1,2,0:T(8,128)}), f32[2,256,256]{1,2,0:T(8,128)}) %all-reduce.29.cloned.1.call-update) | async-done | bytes 524304 | tf_op jit(solution)/shard_map/psum | solution.py:17
  520.3 23.9 %custom-call.66 = f32[2,128,128]{2,1,0:T(8,128)S(1)} custom-call(f32[2,128,128]{2,1,0:T(8,128)S(1)} %cholesky.467), custom_call_target="Cholesky" | custom-call | tf_op jit(solution)/shard_map/jit(cholesky)/cholesky | solution.py:50
  592.5 39.5 %custom-call.69 = f32[2,2,128,128]{2,3,1,0:T(8,128)S(1)} custom-call(f32[2,2,128,128]{3,2,1,0:T(8,128)S(1)} %bitcast.390), custom_call_target="InvertDiagBlocksLowerTriangular" | custom-call | tf_op jit(solution)/shard_map/vmap(jit(_solve_triangular))/triangular_solve | solution.py:51
  638.6 61.7 %all-reduce.31.cloned.1.call-done = f32[2,512,256]{1,2,0:T(8,128)} async-done(((f32[2,512,256]{1,2,0:T(8,128)}), f32[2,512,256]{1,2,0:T(8,128)}) %all-reduce.31.cloned.1.call-update) | async-done | bytes 1048592 | tf_op jit(solution)/shard_map/psum | solution.py:17
  711.1 89.7 %all-reduce.33.cloned.1.call-done = f32[2,1024,256]{1,2,0:T(8,128)} async-done(((f32[2,1024,256]{1,2,0:T(8,128)}), f32[2,1024,256]{1,2,0:T(8,128)}) %all-reduce.33.cloned.1.call-update) | async-done | bytes 2097168 | tf_op jit(solution)/shard_map/psum | solution.py:17
  802.8 61.1 %all-reduce.35.cloned.1.call-done = f32[2,256,256]{1,2,0:T(8,128)} async-done(((f32[2,256,256]{1,2,0:T(8,128)}), f32[2,256,256]{1,2,0:T(8,128)}) %all-reduce.35.cloned.1.call-update) | async-done | bytes 524304 | tf_op jit(solution)/shard_map/psum | solution.py:17
  866.3 23.7 %custom-call.70 = f32[2,128,128]{2,1,0:T(8,128)S(1)} custom-call(f32[2,128,128]{2,1,0:T(8,128)S(1)} %cholesky.470), custom_call_target="Cholesky" | custom-call | tf_op jit(solution)/shard_map/jit(cholesky)/cholesky | solution.py:50
  938.3 39.7 %custom-call.73 = f32[2,2,128,128]{2,3,1,0:T(8,128)S(1)} custom-call(f32[2,2,128,128]{3,2,1,0:T(8,128)S(1)} %bitcast.391), custom_call_target="InvertDiagBlocksLowerTriangular" | custom-call | tf_op jit(solution)/shard_map/vmap(jit(_solve_triangular))/triangular_solve | solution.py:51
  991.8 54.5 %all-reduce.37.cloned.1.call-done = f32[2,512,256]{1,2,0:T(8,128)} async-done(((f32[2,512,256]{1,2,0:T(8,128)}), f32[2,512,256]{1,2,0:T(8,128)}) %all-reduce.37.cloned.1.call-update) | async-done | bytes 1048592 | tf_op jit(solution)/shard_map/psum | solution.py:17
  1072.1 74.7 %all-reduce.39.cloned.1.call-done = f32[2,1024,256]{1,2,0:T(8,128)} async-done(((f32[2,1024,256]{1,2,0:T(8,128)}), f32[2,1024,256]{1,2,0:T(8,128)}) %all-reduce.39.cloned.1.call-update) | async-done | bytes 2097168 | tf_op jit(solution)/shard_map/psum | solution.py:17
  1159.9 50.0 %all-reduce.41.cloned.1.call-done = f32[2,256,256]{1,2,0:T(8,128)} async-done(((f32[2,256,256]{1,2,0:T(8,128)}), f32[2,256,256]{1,2,0:T(8,128)}) %all-reduce.41.cloned.1.call-update) | async-done | bytes 524304 | tf_op jit(solution)/shard_map/psum | solution.py:17
  1284.1 39.5 %custom-call.77 = f32[2,2,128,128]{2,3,1,0:T(8,128)S(1)} custom-call(f32[2,2,128,128]{3,2,1,0:T(8,128)S(1)} %bitcast.392), custom_call_target="InvertDiagBlocksLowerTriangular" | custom-call | tf_op jit(solution)/shard_map/vmap(jit(_solve_triangular))/triangular_solve | solution.py:51
  1330.3 61.7 %all-reduce.43.cloned.1.call-done = f32[2,512,256]{1,2,0:T(8,128)} async-done(((f32[2,512,256]{1,2,0:T(8,128)}), f32[2,512,256]{1,2,0:T(8,128)}) %all-reduce.43.cloned.1.call-update) | async-done | bytes 1048592 | tf_op jit(solution)/shard_map/psum | solution.py:17
  1404.4 35.7 %gather_fusion.6 = f32[2048,512]{1,0:T(8,128)} fusion(f32[2,1024,512]{2,1,0:T(8,128)} %copy.472, s32[2048]{0:T(1024)S(1)} %bitcast.375), kind=kCustom, calls=%fused_computation.6 | custom fusion | bytes 8404992 | tf_op jit(solution)/shard_map/vmap(jit(_take))/gather | solution.py:25
  1564.5 85.4 %gather_fusion.8 = f32[3072,512]{1,0:T(8,128)} fusion(f32[2,1025,512]{2,0,1:T(2,128)} %concatenate.19, s32[3072]{0:T(1024)S(1)} %reshape.1289), kind=kCustom, calls=%fused_computation.8 | custom fusion | bytes 12607488 | tf_op jit(solution)/shard_map/vmap(jit(_take))/gather | solution.py:25
  1676.1 51.0 %gather_fusion.9 = f32[1536,1536]{1,0:T(8,128)} fusion(f32[2,513,1536]{2,0,1:T(2,128)} %concatenate.20, s32[1536]{0:T(1024)S(1)} %reshape.1295), kind=kCustom, calls=%fused_computation.9 | custom fusion | bytes 18886656 | tf_op jit(solution)/shard_map/vmap(jit(_take))/gather | solution.py:25
  1740.2 90.2 %all-reduce.45.cloned.1.call-done = f32[1,1536,256]{1,2,0:T(8,128)} async-done(((f32[1,1536,256]{1,2,0:T(8,128)}), f32[1,1536,256]{1,2,0:T(8,128)}) %all-reduce.45.cloned.1.call-update) | async-done | bytes 1572880 | tf_op jit(solution)/shard_map/psum | solution.py:17
  1832.4 59.8 %all-reduce.47.cloned.1.call-done = f32[1,256,256]{1,2,0:T(8,128)} async-done(((f32[1,256,256]{1,2,0:T(8,128)}), f32[1,256,256]{1,2,0:T(8,128)}) %all-reduce.47.cloned.1.call-update) | async-done | bytes 262160 | tf_op jit(solution)/shard_map/psum | solution.py:17
  1963.8 58.2 %all-reduce.49.cloned.1.call-done = f32[768,256]{0,1:T(8,128)} async-done(((f32[768,256]{0,1:T(8,128)}), f32[768,256]{0,1:T(8,128)}) %all-reduce.49.cloned.1.call-update) | async-done | bytes 786448 | tf_op jit(solution)/shard_map/psum | solution.py:17
  (370 shorter events, 643.8 us)
Async XLA Ops:
  8.0 101.5 %all-reduce.21.cloned.1.call-start = ((), (), s32[]{:S(2)}) async-start(), calls=%async_computation.1 | async-start | bytes 4194304 | tf_op jit(solution)/shard_map/psum | solution.py:17
  16.6 156.0 %all-reduce.23.cloned.1.call-start = ((), (), s32[]{:S(2)}) async-start(), calls=%async_computation.2 | async-start | bytes 1048576 | tf_op jit(solution)/shard_map/psum | solution.py:17
  111.4 243.1 %all-reduce.25.cloned.1.call-start = ((), (), s32[]{:S(2)}) async-start(), calls=%async_computation.3 | async-start | bytes 2097152 | tf_op jit(solution)/shard_map/psum | solution.py:17
  291.1 70.6 %copy-start.4 = (f32[2,1024,256]{1,2,0:T(8,128)}, f32[2,1024,256]{1,2,0:T(8,128)S(1)}, u32[]{:S(2)}) copy-start(f32[2,1024,256]{1,2,0:T(8,128)S(1)} %convolution_select_fusion.4) | copy-start | bytes 6291460
  292.7 162.3 %all-reduce.27.cloned.1.call-start = ((), (), s32[]{:S(2)}) async-start(), calls=%async_computation.4 | async-start | bytes 4194304 | tf_op jit(solution)/shard_map/psum | solution.py:17
  365.2 152.7 %all-reduce.29.cloned.1.call-start = ((), (), s32[]{:S(2)}) async-start(), calls=%async_computation.5 | async-start | bytes 1048576 | tf_op jit(solution)/shard_map/psum | solution.py:17
  456.9 243.4 %all-reduce.31.cloned.1.call-start = ((), (), s32[]{:S(2)}) async-start(), calls=%async_computation.6 | async-start | bytes 2097152 | tf_op jit(solution)/shard_map/psum | solution.py:17
  636.8 70.7 %copy-start.6 = (f32[2,1024,256]{1,2,0:T(8,128)}, f32[2,1024,256]{1,2,0:T(8,128)S(1)}, u32[]{:S(2)}) copy-start(f32[2,1024,256]{1,2,0:T(8,128)S(1)} %convolution_select_fusion.3) | copy-start | bytes 6291460
  638.5 162.3 %all-reduce.33.cloned.1.call-start = ((), (), s32[]{:S(2)}) async-start(), calls=%async_computation.7 | async-start | bytes 4194304 | tf_op jit(solution)/shard_map/psum | solution.py:17
  711.0 152.9 %all-reduce.35.cloned.1.call-start = ((), (), s32[]{:S(2)}) async-start(), calls=%async_computation.8 | async-start | bytes 1048576 | tf_op jit(solution)/shard_map/psum | solution.py:17
  802.7 243.6 %all-reduce.37.cloned.1.call-start = ((), (), s32[]{:S(2)}) async-start(), calls=%async_computation.9 | async-start | bytes 2097152 | tf_op jit(solution)/shard_map/psum | solution.py:17
  982.8 70.7 %copy-start.7 = (f32[2,1024,256]{1,2,0:T(8,128)}, f32[2,1024,256]{1,2,0:T(8,128)S(1)}, u32[]{:S(2)}) copy-start(f32[2,1024,256]{1,2,0:T(8,128)S(1)} %convolution_select_fusion.2) | copy-start | bytes 6291460
  984.5 79.8 %sort.39.cloned.1.call-start = ((), (), s32[]{:S(2)}) async-start(), calls=%async_computation.17 | async-start | bytes 393248 | tf_op jit(solution)/shard_map/jit(argsort)/sort | solution.py:96
  986.2 81.5 %sort.37.cloned.1.call-start = ((), (), s32[]{:S(2)}) async-start(), calls=%async_computation.16 | async-start | bytes 393248 | tf_op jit(solution)/shard_map/jit(argsort)/sort | solution.py:97
  987.5 159.3 %all-reduce.39.cloned.1.call-start = ((), (), s32[]{:S(2)}) async-start(), calls=%async_computation.10 | async-start | bytes 4194304 | tf_op jit(solution)/shard_map/psum | solution.py:17
  1057.0 152.9 %all-reduce.41.cloned.1.call-start = ((), (), s32[]{:S(2)}) async-start(), calls=%async_computation.11 | async-start | bytes 1048576 | tf_op jit(solution)/shard_map/psum | solution.py:17
  1148.7 243.2 %all-reduce.43.cloned.1.call-start = ((), (), s32[]{:S(2)}) async-start(), calls=%async_computation.12 | async-start | bytes 2097152 | tf_op jit(solution)/shard_map/psum | solution.py:17
  1328.5 70.4 %copy-start.8 = (f32[2,1024,256]{1,2,0:T(8,128)}, f32[2,1024,256]{1,2,0:T(8,128)S(1)}, u32[]{:S(2)}) copy-start(f32[2,1024,256]{1,2,0:T(8,128)S(1)} %convolution_select_fusion.1) | copy-start | bytes 6291460
  1477.9 61.0 %all-to-all-start = ((f32[128,2,128,32]{2,3,1,0:T(8,128)}), f32[128,2,128,32]{2,3,1,0:T(8,128)}, u32[]{:S(2)}, u32[]{:S(2)}) async-start(f32[128,2,128,32]{2,3,1,0:T(8,128)} %bitcast.384), calls=%async_computation | async-start | bytes 8388608 | tf_op jit(solution)/shard_map/all_to_all | solution.py:130
  1486.4 343.9 %all-reduce.45.cloned.1.call-start = ((), (), s32[]{:S(2)}) async-start(), calls=%async_computation.13 | async-start | bytes 3145728 | tf_op jit(solution)/shard_map/psum | solution.py:17
  1497.6 17.8 copy-start.14
  1497.6 18.2 copy-start.12
  1740.1 152.1 %all-reduce.47.cloned.1.call-start = ((), (), s32[]{:S(2)}) async-start(), calls=%async_computation.14 | async-start | bytes 524288 | tf_op jit(solution)/shard_map/psum | solution.py:17
  1832.1 190.0 %all-reduce.49.cloned.1.call-start = ((), (), s32[]{:S(2)}) async-start(), calls=%async_computation.15 | async-start | bytes 1572864 | tf_op jit(solution)/shard_map/psum | solution.py:17
  (9 other events, 40.3 us)
Sparse Core Ops, SparseCore 0:
  16.7 92.7 all-reduce.20
  112.6 60.0 all-reduce.22
  292.9 61.5 all-reduce.24
  365.4 89.5 all-reduce.26
  457.9 60.0 all-reduce.28
  638.7 61.5 all-reduce.30
  711.2 89.6 all-reduce.32
  803.8 60.0 all-reduce.34
  984.6 61.6 all-reduce.36
  1057.1 89.6 all-reduce.38
  1149.8 60.0 all-reduce.40
  1330.3 61.5 all-reduce.42
  1740.3 90.0 all-reduce.44
  1833.1 59.0 all-reduce.46
  1961.3 60.6 all-reduce.48
Sparse Core Ops, SparseCore 1:
  988.0 6.9 sort.43.cloned.1.call-done
  997.5 9.7 sort.41.cloned.1.call-done
  (2 shorter events, 0.0 us)
where the time goes:
time: 2060 us; the launch traced here: 2050 us
  waiting for transfers between devices  1030 us (50%)
  other arithmetic  548 us (27%)
  local copies, waits for them, and re-layouts  376 us (18%)
  matrix products  67.7 us (3%)
    psum x15, waiting for transfers between devices, from_root(): return lax.psum(kept, axis)  1030 us
    another operation x40, other arithmetic, eliminate(): factor = jnp.linalg.cholesky(corner)  303 us
    gather x8, local copies, waits for them, and re-layouts, take_rows(): jnp.take(single, picks, axis=0)  209 us
    another operation x12, other arithmetic, eliminate(): jax.vmap(partial(jax.scipy.linalg.solve_triangular, lower=True))  179 us
    dot_general x5, matrix products, outer_update(): jnp.einsum('kin,kjn->kij', factor_rows, crossed, precision=exact_mode)  41.4 us
  transfers between devices with their start and end apart: 16, of which 15 were waited for; matrix products, arithmetic and copies ran while one was open for 4% of the time, Pallas kernels for 0%

commit v1 on v0

v1 whole, which is shorter than its diff:
```python
from functools import partial

import jax
import jax.numpy as jnp
from jax import lax
from jax.experimental import pallas as pl
from jax.experimental.pallas import tpu as pltpu
from jax.sharding import PartitionSpec as P

F32 = jnp.float32
BF16 = jnp.bfloat16
NB = 256
SB = 64
GROUP = 4
BLK = 512
KEYS = 16
HIGHEST = lax.Precision.HIGHEST
VMEM_LIMIT = 56 << 20


def mm(a, b, ca, cb):
    return lax.dot_general(
        a, b, (((ca,), (cb,)), ((), ())), precision=HIGHEST, preferred_element_type=F32
    )


def mm_bf(a, b, ca, cb):
    return lax.dot_general(a, b, (((ca,), (cb,)), ((), ())), preferred_element_type=F32)


def split3(x):
    hi = x.astype(BF16)
    rest = x - hi.astype(F32)
    mid = rest.astype(BF16)
    low = (rest - mid.astype(F32)).astype(BF16)
    return hi, mid, low


def call(kernel, name, **kw):
    return pl.pallas_call(
        kernel,
        name=name,
        compiler_params=pltpu.CompilerParams(vmem_limit_bytes=VMEM_LIMIT),
        **kw,
    )


def factor_small(diag):
    n = SB
    ri = lax.broadcasted_iota(jnp.int32, (n, n), 0)
    ci = lax.broadcasted_iota(jnp.int32, (n, n), 1)
    full = jnp.concatenate([diag, jnp.where(ri == ci, 1.0, 0.0)], axis=1)
    nv = n // 8
    rows = [full[8 * v : 8 * v + 8, :] for v in range(nv)]
    sub = lax.broadcasted_iota(jnp.int32, (8, 2 * n), 0)
    wide = lambda x: jnp.broadcast_to(x, (8, 2 * n))
    pivots = []
    for j0 in range(0, n, GROUP):
        v0 = j0 // 8
        cols = [[wide(rows[v][:, j0 + q : j0 + q + 1]) for v in range(v0, nv)] for q in range(GROUP)]
        at = [(j0 + q) % 8 for q in range(GROUP)]
        lead = [wide(rows[v0][at[q] : at[q] + 1, :]) for q in range(GROUP)]
        for q in range(GROUP):
            inv = 1.0 / wide(cols[q][0][at[q] : at[q] + 1, :])
            pivots.append(inv)
            scaled = lead[q] * inv
            below = [jnp.where(sub > at[q], cols[q][0], 0.0)] + cols[q][1:]
            for t in range(q + 1, GROUP):
                ratio = wide(cols[t][0][at[q] : at[q] + 1, :]) * inv
                weight = wide(cols[q][0][at[t] : at[t] + 1, :])
                cols[t] = [cols[t][i] - below[i] * ratio for i in range(len(below))]
                lead[t] = lead[t] - weight * scaled
            for i in range(len(below)):
                rows[v0 + i] = rows[v0 + i] - below[i] * scaled
    out = []
    for v in range(nv):
        scale = pivots[8 * v]
        for s in range(1, 8):
            scale = jnp.where(sub == s, pivots[8 * v + s], scale)
        out.append(rows[v] * jnp.sqrt(scale))
    return jnp.concatenate(out, axis=0)


def factor_diag(d_ref, w_ref, base):
    ri = lax.broadcasted_iota(jnp.int32, (NB, NB), 0)
    ci = lax.broadcasted_iota(jnp.int32, (NB, NB), 1)
    w_ref[...] = jnp.where(ri == ci, 1.0, 0.0)
    cb = lax.broadcasted_iota(jnp.int32, (SB, NB), 1)
    rb = lax.broadcasted_iota(jnp.int32, (SB, NB), 0)
    for lo in range(0, NB, SB):
        hi = lo + SB
        strip = d_ref[base + lo : base + hi, base : base + NB]
        small = factor_small(strip[:, lo:hi])
        both = mm(small[:, SB:], jnp.concatenate([strip, w_ref[lo:hi, :]], axis=1), 1, 0)
        up = jnp.where(cb >= rb + lo, both[:, :NB], 0.0)
        inv = jnp.where(cb <= rb + lo, both[:, NB:], 0.0)
        d_ref[base + lo : base + hi, base : base + NB] = up
        w_ref[lo:hi, :] = inv
        if hi < NB:
            update = mm(up[:, hi:], jnp.concatenate([up, inv], axis=1), 0, 0)
            d_ref[base + hi : base + NB, base : base + NB] -= update[:, :NB]
            w_ref[hi:, :] -= update[:, NB:]


def factor_all(n, u_ref, w_ref):
    for lo in range(0, n, NB):
        hi = lo + NB
        factor_diag(u_ref, w_ref.at[lo // NB], lo)
        if hi < n:
            right = mm(w_ref[lo // NB], u_ref[lo:hi, hi:], 1, 0)
            u_ref[lo:hi, hi:] = right
            u_ref[hi:, hi:] -= mm(right, right, 0, 0)
    for lo in range(NB, n, NB):
        u_ref[lo : lo + NB, :lo] = jnp.zeros((NB, lo), F32)


def chol_kernel(n, a_ref, u_ref, w_ref):
    u_ref[...] = a_ref[...]
    factor_all(n, u_ref, w_ref)


def cholesky_upper(a, name):
    n = a.shape[0]
    return call(
        partial(chol_kernel, n),
        name,
        out_shape=(
            jax.ShapeDtypeStruct((n, n), F32),
            jax.ShapeDtypeStruct((n // NB, NB, NB), F32),
        ),
    )(a)


def one_hot(pos_row, n):
    ids = lax.broadcasted_iota(jnp.int32, (n, pos_row.shape[1]), 0)
    return jnp.where(ids == pos_row, 1.0, 0.0).astype(BF16)


def pack_x_kernel(flag_ref, pos_ref, f_ref, o_ref):
    pivot = flag_ref[0] != 0

    @pl.when(pivot)
    def _():
        for y in range(4):
            for q in range(4):
                o_ref[y, 0, q * NB : (q + 1) * NB, :] = f_ref[
                    0, y * NB : (y + 1) * NB, q * 128 : (q + 1) * 128
                ]

    @pl.when(jnp.logical_not(pivot))
    def _():
        place = one_hot(pos_ref[0], BLK)
        out = sum(mm_bf(part, place, 1, 1) for part in split3(f_ref[0]))
        for y in range(4):
            o_ref[y, 0] = out[:, y * 128 : (y + 1) * 128]


def pack_kernel(flag_ref, pos_ref, f_ref, o_ref):
    pivot = flag_ref[0] != 0
    for b in range(2):
        place_row = one_hot(pos_ref[0, b : b + 1, :], BLK)
        parts = split3(f_ref[0, b * BLK : (b + 1) * BLK, :])
        rows = [mm_bf(place_row, part, 1, 0) for part in parts]

        def store(total):
            for y in range(4):
                for p in range(KEYS):
                    o_ref[y, 0, p, b * 32 : (b + 1) * 32, :] = total[
                        p * 32 : (p + 1) * 32, y * 128 : (y + 1) * 128
                    ]

        @pl.when(pivot)
        def _():
            store(rows[0] + rows[1] + rows[2])

        @pl.when(jnp.logical_not(pivot))
        def _():
            place_col = one_hot(pos_ref[0, 2:3, :], BLK)
            store(sum(mm_bf(place_col, row.astype(BF16), 1, 1) for row in rows))


def chol_gathered_kernel(a_ref, u_ref, w_ref):
    for yy in range(4):
        for pc in range(KEYS):
            q, i = pc // 4, pc % 4
            for h in range(2):
                u_ref[
                    yy * NB + i * 64 : yy * NB + i * 64 + 64,
                    h * BLK + q * 128 : h * BLK + q * 128 + 128,
                ] = a_ref[yy * KEYS + pc, h]
    factor_all(u_ref.shape[0], u_ref, w_ref)


def panel_kernel(u_ref, w_ref, y_ref, x_ref, c_ref, rx_ref, s_ref, ry_ref):
    step = pl.program_id(0)
    panels = u_ref.shape[0] // NB

    @pl.when(step == 0)
    def _():
        for p in range(panels):
            lanes = [(2 * p + t) // 4 for t in range(2)]
            which = [(2 * p + t) % 4 for t in range(2)]
            cur = jnp.concatenate(
                [y_ref[which[t], :, lanes[t]].reshape(448, 128) for t in range(2)], axis=1
            )
            if p:
                cur = cur - mm(ry_ref[:, : p * NB], u_ref[: p * NB, p * NB : (p + 1) * NB], 1, 0)
            ry_ref[:, p * NB : (p + 1) * NB] = mm(cur, w_ref[p], 1, 1)

    for p in range(panels):
        lo, hi = p * NB, (p + 1) * NB
        cur = jnp.concatenate([x_ref[0, lo:hi, :], x_ref[1, lo:hi, :]], axis=1)
        if p:
            cur = cur - mm(u_ref[:lo, lo:hi], rx_ref[:lo, :], 0, 0)
        rx_ref[lo:hi, :] = mm(w_ref[p], cur, 1, 0)
    prod = mm(ry_ref[...], rx_ref[...], 1, 0)
    c0 = c_ref[0, 2:, 0:32, :].reshape(448, 128) - prod[:, :128]
    c1 = c_ref[0, 2:, 32:64, :].reshape(448, 128) - prod[:, 128:]
    lane = lax.broadcasted_iota(jnp.int32, (448, 128), 1)
    s_ref[0] = jnp.where(lane < 64, c0, pltpu.roll(c1, 64, 1))
    s_ref[1] = jnp.where(lane < 64, pltpu.roll(c0, 64, 1), c1)


def unpack_kernel(src_ref, r_ref, o_ref):
    for k in range(2):
        wide = jnp.concatenate([r_ref[2 * yy + k] for yy in range(4)], axis=1)
        place = one_hot_rows(src_ref[k], 1024)
        o_ref[k] = sum(mm_bf(place, part, 1, 1) for part in split3(wide))


def one_hot_rows(src_col, n):
    ids = lax.broadcasted_iota(jnp.int32, (src_col.shape[0], n), 1)
    return jnp.where(ids == src_col, 1.0, 0.0).astype(BF16)


def merge_kernel(tx_ref, ty_ref, s_ref, p_ref, o_ref, part_ref, ey_ref):
    tile = pl.program_id(0)

    @pl.when(tile == 0)
    def _():
        for k in range(2):
            ey_ref[k] = one_hot(ty_ref[k], 768)
            for i, part in enumerate(split3(s_ref[k])):
                part_ref[k, i] = part

    acc = p_ref[...]
    for k in range(2):
        ex = one_hot(tx_ref[k] - tile * NB, NB)
        for i in range(3):
            half = mm_bf(ex, part_ref[k, i], 1, 1)
            acc = acc + mm_bf(half.astype(BF16), ey_ref[k], 1, 1)
    o_ref[...] = acc


def final_kernel(flag_ref, w_ref, m_ref, row_ref, col_ref, o_ref, f_ref, rc_ref):
    tile = pl.program_id(0)

    @pl.when(tile == 0)
    def _():
        rc_ref[...] = mm(w_ref[0], col_ref[...], 1, 0)

    rows = mm(row_ref[...], w_ref[0], 1, 1)
    f_ref[...] = rows
    out = m_ref[...] - mm(rows, rc_ref[...], 1, 0)
    lane = lax.broadcasted_iota(jnp.int32, out.shape, 1)
    keep_row = jnp.logical_or(flag_ref[0] != 0, tile > 0)
    keep = jnp.logical_and(keep_row, jnp.logical_or(flag_ref[1] != 0, lane >= NB))
    o_ref[...] = jnp.where(keep, out, 0.0)


def smem():
    return pl.BlockSpec(memory_space=pltpu.SMEM)


def whole(shape):
    return pl.BlockSpec(shape, lambda *_: (0,) * len(shape))


def local(child_fronts, parent_front, child_map):
    r = lax.axis_index("row")
    c = lax.axis_index("col")
    core = r % 2
    y = r // 2
    nblk = child_map.shape[1] // BLK
    parity = [[(2 * i + k) * KEYS + j for i in range(4) for j in range(KEYS)] for k in range(2)]
    parity_row = [[2 * i + k for i in range(4)] for k in range(2)]

    maps = child_map.reshape(2 * nblk, BLK)
    keys = maps // 768
    hot = (keys[:, :, None] == jnp.arange(KEYS, dtype=jnp.int32)).astype(BF16)
    lower = (jnp.arange(BLK)[:, None] >= jnp.arange(BLK)[None, :]).astype(BF16)
    counts = jnp.einsum("ef,bfk->bek", lower, hot, preferred_element_type=F32)
    rank = jnp.sum(counts * hot.astype(F32), axis=2).astype(jnp.int32) - 1
    pos = (keys * 32 + rank).reshape(2, nblk, BLK)
    maps = maps.reshape(2, nblk, BLK)

    pos_c = lax.dynamic_slice_in_dim(pos, jnp.maximum(c - 2, 0), 1, axis=1)
    pos_r = lax.dynamic_slice_in_dim(pos, jnp.maximum(2 * r - 2, 0), 2, axis=1)
    flag = (c < 2).astype(jnp.int32)[None]

    packed_x = call(
        pack_x_kernel,
        "pack_x",
        grid=(2,),
        in_specs=[
            smem(),
            pl.BlockSpec((1, 1, BLK), lambda k: (k, 0, 0)),
            pl.BlockSpec((1, 1024, BLK), lambda k: (k, 0, 0)),
        ],
        out_specs=pl.BlockSpec((4, 1, 1024, 128), lambda k: (0, k, 0, 0)),
        out_shape=jax.ShapeDtypeStruct((4, 2, 1024, 128), F32),
    )(flag, pos_c, child_fronts)
    own = packed_x[0, 0]
    for dest in range(1, 8):
        got = lax.ppermute(packed_x[dest // 2, dest % 2], "row", [(0, dest)])
        own = jnp.where(r == dest, got, own)

    spread = lax.all_to_all(own.reshape(KEYS, 64, 128), "col", split_axis=0, concat_axis=0, tiled=True)
    pieces = lax.all_gather(spread[:2], ("row", "col"), axis_index_groups=parity)
    upper, inverses = call(
        chol_gathered_kernel,
        "child_factor",
        out_shape=(
            jax.ShapeDtypeStruct((1024, 1024), F32),
            jax.ShapeDtypeStruct((4, NB, NB), F32),
        ),
    )(pieces)
    own, pieces = lax.optimization_barrier((own, spread))
    panel_x = lax.all_gather(own, "col")

    packed = call(
        pack_kernel,
        "pack",
        grid=(2,),
        in_specs=[
            smem(),
            pl.BlockSpec((1, 3, BLK), lambda k: (k, 0, 0)),
            pl.BlockSpec((1, 1024, BLK), lambda k: (k, 0, 0)),
        ],
        out_specs=pl.BlockSpec((4, 1, KEYS, 64, 128), lambda k: (0, k, 0, 0, 0)),
        out_shape=jax.ShapeDtypeStruct((4, 2, KEYS, 64, 128), F32),
    )(flag, jnp.concatenate([pos_r, pos_c], axis=1), child_fronts)
    arrived = lax.all_to_all(
        packed.reshape(8 * KEYS, 64, 128), ("row", "col"), split_axis=0, concat_axis=0, tiled=True
    ).reshape(8, KEYS, 64, 128)
    panel_y = lax.all_gather(arrived[1:, :2], "row", axis_index_groups=parity_row)

    factor_x, schur = call(
        panel_kernel,
        "panel",
        grid=(7,),
        in_specs=[
            whole((1024, 1024)),
            whole((4, NB, NB)),
            whole((4, 7, 2, 64, 128)),
            pl.BlockSpec((pl.Element(2), pl.Element(1024), pl.Element(128)), lambda g: (2 * g + 2, 0, 0)),
            pl.BlockSpec((1, KEYS, 64, 128), lambda g: (g + 1, 0, 0, 0)),
        ],
        out_specs=(
            pl.BlockSpec((1024, NB), lambda g: (0, g)),
            pl.BlockSpec((2, 448, 128), lambda g: (0, 0, g)),
        ),
        out_shape=(
            jax.ShapeDtypeStruct((1024, 1792), F32),
            jax.ShapeDtypeStruct((2, 448, 896), F32),
        ),
        scratch_shapes=[pltpu.VMEM((448, 1024), F32)],
    )(upper, inverses, panel_y, panel_x, arrived)

    mine = lax.dynamic_index_in_dim(schur, core, 0, keepdims=False)
    other = lax.dynamic_index_in_dim(schur, 1 - core, 0, keepdims=False)
    got = lax.ppermute(other, "row", [(i, i ^ 1) for i in range(8)])
    first = core == 0
    both = jnp.stack([jnp.where(first, mine, got), jnp.where(first, got, mine)])

    strip = lax.dynamic_slice_in_dim(factor_x, c * 64, 64, axis=0)
    head = lax.dynamic_slice(upper, (c * 64, y * NB), (64, NB))
    outgoing = jnp.concatenate([head[None], jnp.stack(jnp.split(strip, 7, axis=1))])
    landed = lax.all_to_all(outgoing, "row", split_axis=0, concat_axis=0, tiled=True)
    spot = (pos_r // 128) * NB + jnp.arange(2, dtype=jnp.int32)[None, :, None] * 128 + pos_r % 128
    natural = jnp.broadcast_to(jnp.arange(1024, dtype=jnp.int32), (2, 1024))
    spot = jnp.where(r == 0, natural, spot.reshape(2, 1024))
    child_factor = call(
        unpack_kernel, "unpack", out_shape=jax.ShapeDtypeStruct((2, 1024, 64), F32)
    )(spot[:, :, None], landed)

    def sorted_maps(start, count):
        ids = start + jnp.arange(count, dtype=jnp.int32)
        return jnp.sum(
            jnp.where(pos[:, :, :, None] == ids, maps[:, :, :, None], 0), axis=2, dtype=jnp.int32
        )

    to_rows = sorted_maps(r * 64, 64).reshape(2, 1, 896) - r * 1536
    to_cols = sorted_maps(c * 32, 32).reshape(2, 1, 448) - c * 768
    merged = call(
        merge_kernel,
        "merge",
        grid=(6,),
        in_specs=[
            whole((2, 1, 896)),
            whole((2, 1, 448)),
            whole((2, 448, 896)),
            pl.BlockSpec((NB, 768), lambda t: (t, 0)),
        ],
        out_specs=pl.BlockSpec((NB, 768), lambda t: (t, 0)),
        out_shape=jax.ShapeDtypeStruct((1536, 768), F32),
        scratch_shapes=[pltpu.VMEM((2, 3, 448, 896), BF16), pltpu.VMEM((2, 768, 448), BF16)],
    )(to_rows, to_cols, both, parent_front)

    down = lax.all_to_all(merged[:NB].reshape(8, 32, 768), "row", split_axis=0, concat_axis=0, tiled=True)
    top = lax.all_gather(down[0], "row").reshape(NB, 768)
    side = jnp.concatenate([merged[:, :NB], top[:, :NB]]).reshape(KEYS, 112, NB)
    across = lax.all_to_all(side, "col", split_axis=0, concat_axis=0, tiled=True)
    left = lax.all_gather(across[0], "col").reshape(1792, NB)
    _, parent_inverse = cholesky_upper(left[1536:], "parent_factor")
    schur_out, rows_out = call(
        final_kernel,
        "final",
        grid=(6,),
        in_specs=[
            smem(),
            whole((1, NB, NB)),
            pl.BlockSpec((NB, 768), lambda t: (t, 0)),
            pl.BlockSpec((NB, NB), lambda t: (t, 0)),
            whole((NB, 768)),
        ],
        out_specs=(
            pl.BlockSpec((NB, 768), lambda t: (t, 0)),
            pl.BlockSpec((NB, NB), lambda t: (t, 0)),
        ),
        out_shape=(
            jax.ShapeDtypeStruct((1536, 768), F32),
            jax.ShapeDtypeStruct((1536, NB), F32),
        ),
        scratch_shapes=[pltpu.VMEM((NB, 768), F32)],
    )(jnp.stack([r, c]), parent_inverse, merged, left, top)
    parent_factor = lax.dynamic_slice_in_dim(rows_out, c * 16, 16, axis=1)
    return child_factor, parent_factor, schur_out


def solution(mesh):
    return jax.shard_map(
        local,
        mesh=mesh,
        in_specs=(P(None, "row", "col"), P("row", "col"), P()),
        out_specs=(P(None, "row", "col"), P("row", "col"), P("row", "col")),
        check_vma=False,
    )
```

time: 2060 us -> 517 us (0.25)
  waiting for transfers between devices: 1030 us -> 106 us
  other arithmetic: 548 us -> 10.4 us
  local copies, waits for them, and re-layouts: 376 us -> 34.9 us
  Pallas kernels: 0 us -> 192 us
  blocking collectives: 0 us -> 127 us
  matrix products: 67.7 us -> 0.54 us
    psum x15 -> x0, waiting for transfers between devices: 1030 us -> none  [from_root(): return lax.psum(kept, axis)]
    another operation x52 -> x3, other arithmetic: 481 us -> 4.1 us  [the longest x2 3.51 us: local(): both = jnp.stack([jnp.where(first, mine, got), jnp.where(first, got, mine)])]
    gather x23 -> x0, local copies, waits for them, and re-layouts: 257 us -> none  [the longest x8 209 us: take_rows(): jnp.take(single, picks, axis=0)]
    pallas_call x0 -> x8, Pallas kernels: none -> 192 us  [the longest x1 64.1 us: local(): call(chol_gathered_kernel, 'child_factor', out_shape=(jax.ShapeDtypeStruc...]
    all_to_all x0 -> x3, blocking collectives: none -> 114 us  [the longest x1 61.8 us: local(): lax.all_to_all(packed.reshape(8 * KEYS, 64, 128), ('row', 'col'), split_a...]
    all_gather x0 -> x4, waiting for transfers between devices: none -> 69.1 us  [the longest x1 37.4 us: local(): panel_x = lax.all_gather(own, 'col')]
    dot_general x10 -> x1, matrix products: 58.9 us -> 0.54 us  [local(): counts = jnp.einsum('ef,bfk->bek', lower, hot, preferred_element_type=F32)]
    select_n x28 -> x3, other arithmetic: 48.3 us -> 2.3 us  [the longest x1 1.25 us: local(): own = jnp.where(r == dest, got, own)]
  transfers between devices with their start and end apart: 16 -> 14, of which waited for: 15 -> 10; matrix products, arithmetic and copies ran while one was open for 4% -> 4% of each run, Pallas kernels for 0% -> 15%
where the time goes in v1:
time: 517 us; the launch traced here: 509 us
  Pallas kernels  192 us (37%)
  blocking collectives  127 us (25%)
  waiting for transfers between devices  106 us (21%)
  local copies, waits for them, and re-layouts  34.9 us (7%)
  starting transfers between devices  24.2 us (5%)
  between operations  14.5 us (3%)
  other arithmetic  10.4 us (2%)
    pallas_call x1, Pallas kernels, local(): call(chol_gathered_kernel, 'child_factor', out_shape=(jax.ShapeDtypeStruc...  64.1 us
    all_to_all x1, blocking collectives, local(): lax.all_to_all(packed.reshape(8 * KEYS, 64, 128), ('row', 'col'), split_a...  61.8 us
    pallas_call x1, Pallas kernels, local(): call(panel_kernel, 'panel', grid=(7,), in_specs=[whole((1024, 1024)), who...  56.2 us
    all_gather x1, waiting for transfers between devices, local(): panel_x = lax.all_gather(own, 'col')  37.4 us
    all_to_all x1, blocking collectives, local(): lax.all_to_all(side, 'col', split_axis=0, concat_axis=0, tiled=True)  31.2 us
    pallas_call x1, Pallas kernels, local(): call(merge_kernel, 'merge', grid=(6,), in_specs=[whole((2, 1, 896)), whol...  26.3 us
    all_gather x1, waiting for transfers between devices, local(): lax.all_gather(spread[:2], ('row', 'col'), axis_index_groups=parity)  25.6 us
    all_to_all x1, blocking collectives, local(): lax.all_to_all(own.reshape(KEYS, 64, 128), 'col', split_axis=0, concat_ax...  20.7 us
  transfers between devices with their start and end apart: 14, of which 10 were waited for; matrix products, arithmetic and copies ran while one was open for 4% of the time, Pallas kernels for 15%

profile of v1, /device:TPU:0, one launch (start us, length us, event | category | flops | bytes accessed | tf_op | source)
XLA Modules:
  0.0 509.1 jit_solution(17233096822618843222)
XLA Ops:
  11.3 3.7 pack_x.1
  17.3 4.5 collective-permute-start
  31.5 2.5 collective-permute-done.1
  36.7 5.6 %collective-permute-done.4 = f32[1024,128]{1,0:T(8,128)} collective-permute-done((f32[1024,128]{1,0:T(8,128)S(1)}, f32[1024,128]{1,0:T(8,128)}, u32[]{:S(2)}, u32[]{:S(2)}) %collective-permute-start.4) | collective-permute-done | bytes 524320 | tf_op jit(solution)/shard_map/ppermute | solution.py:315
  42.4 5.6 %collective-permute-done.5 = f32[1024,128]{1,0:T(8,128)} collective-permute-done((f32[1024,128]{1,0:T(8,128)S(1)}, f32[1024,128]{1,0:T(8,128)}, u32[]{:S(2)}, u32[]{:S(2)}) %collective-permute-start.5) | collective-permute-done | bytes 524320 | tf_op jit(solution)/shard_map/ppermute | solution.py:315
  49.2 20.7 %all_to_all.25 = f32[16,64,128]{2,1,0:T(8,128)S(1)} all-to-all(f32[16,64,128]{2,1,0:T(8,128)S(1)} %bitcast.100), channel_id=1, replica_groups=mesh['row'=8,'col'=16] {'col'}, dimensions={0} | all-to-all | bytes 1048576 | tf_op jit(solution)/shard_map/all_to_all | solution.py:318
  71.3 7.6 %pack.1 = f32[4,2,16,64,128]{4,3,2,1,0:T(8,128)} custom-call(s32[1]{0:T(128)} %bitcast.2.flag_ref, s32[2,3,512]{2,1,0:T(4,128)} %pad_add_fusion.pos_ref, f32[2,1024,512]{2,1,0:T(8,128)} %f_ref.3), custom_call_target="tpu_custom_call" | custom-call | tf_op jit(solution)/shard_map/pack/pallas_call | solution.py:331
  78.9 61.8 %all_to_all.26 = f32[128,64,128]{2,1,0:T(8,128)S(1)} all-to-all(f32[128,64,128]{2,1,0:T(8,128)} %bitcast.97), channel_id=1, replica_groups=mesh['row'=8,'col'=16] {'row','col'}, dimensions={0} | all-to-all | bytes 8388608 | tf_op jit(solution)/shard_map/all_to_all | solution.py:343
  144.3 25.6 %all-gather.10.cloned.1.call-done = f32[128,64,128]{2,1,0:T(8,128)} async-done(((f32[2,64,128]{2,1,0:T(8,128)}), f32[128,64,128]{2,1,0:T(8,128)}) %all-gather.10.cloned.1.call-update) | async-done | bytes 4194320 | tf_op jit(solution)/shard_map/all_gather | solution.py:319
  169.9 64.1 %child_factor.1 = (f32[1024,1024]{1,0:T(8,128)}, f32[4,256,256]{2,1,0:T(8,128)}) custom-call(f32[64,2,64,128]{3,2,1,0:T(8,128)} %bitcast.103), custom_call_target="tpu_custom_call" | custom-call | tf_op jit(solution)/shard_map/child_factor/pallas_call | solution.py:320
  234.0 37.4 %all-gather.14.cloned.1.call-done = f32[16384,128]{1,0:T(8,128)} async-done(((f32[1024,128]{1,0:T(8,128)}), f32[16384,128]{1,0:T(8,128)}) %all-gather.14.cloned.1.call-update) | async-done | bytes 8388624 | tf_op jit(solution)/shard_map/all_gather | solution.py:329
  271.4 56.2 %panel.1 = (f32[1024,1792]{1,0:T(8,128)}, f32[2,448,896]{2,1,0:T(8,128)}) custom-call(f32[1024,1024]{1,0:T(8,128)} %get-tuple-element.11.u_ref, f32[4,256,256]{2,1,0:T(8,128)} %get-tuple-element.12.w_ref, f32[4,7,2,64,128]{4,3,2,1,0:T(8,128)} %bitcast.106, f32[16,1024,128]{2,1,0:T(8,128)} %bitcast.98, f32[8,16,64,128]{3,2,1,0:T(8,128)} %bitcast.96), custom_call_target="tpu_custom_call" | custom-call | tf_op jit(solution)/shard_map/panel/pallas_call | solution.py:348
  327.6 2.9 dynamic-slice_bitcast_fusion
  338.0 26.3 %merge.1.m_ref = f32[1536,768]{1,0:T(8,128)} custom-call(s32[2,1,896]{2,1,0:T(1,128)} %sub.64.tx_ref, s32[2,1,448]{2,1,0:T(1,128)} %sub.65.ty_ref, f32[2,448,896]{2,1,0:T(8,128)} %pad_maximum_fusion.s_ref, f32[1536,768]{1,0:T(8,128)} %p_ref.1), custom_call_target="tpu_custom_call" | custom-call | tf_op jit(solution)/shard_map/merge/pallas_call | solution.py:395
  366.4 4.4 all-to-all-start.3
  370.8 13.1 %all-to-all-done.3 = f32[8,32,768]{2,1,0:T(8,128)S(1)} async-done(((f32[8,32,768]{2,1,0:T(8,128)}), f32[8,32,768]{2,1,0:T(8,128)S(1)}, u32[]{:S(2)}, u32[]{:S(2)}) %all-to-all-start.3) | async-done | bytes 786464 | tf_op jit(solution)/shard_map/all_to_all | solution.py:410
  384.0 13.5 %all_gather.30 = f32[8,32,768]{2,1,0:T(8,128)S(1)} all-gather(f32[1,32,768]{2,1,0:T(8,128)S(1)} %slice.76), channel_id=1, replica_groups=mesh['row'=8,'col'=16] {'row'}, dimensions={0}, use_global_device_ids=true | all-gather | bytes 884736 | tf_op jit(solution)/shard_map/all_gather | solution.py:411
  397.6 31.2 %all_to_all.27 = f32[16,112,256]{2,1,0:T(8,128)S(1)} all-to-all(f32[16,112,256]{2,1,0:T(8,128)S(1)} %bitcast.99), channel_id=1, replica_groups=mesh['row'=8,'col'=16] {'col'}, dimensions={0} | all-to-all | bytes 3670016 | tf_op jit(solution)/shard_map/all_to_all | solution.py:413
  441.2 3.7 all-to-all-start.2
  447.6 7.7 %all-to-all-done.2.r_ref = f32[8,64,256]{2,1,0:T(8,128)S(1)} async-done(((f32[8,64,256]{2,1,0:T(8,128)}), f32[8,64,256]{2,1,0:T(8,128)S(1)}, u32[]{:S(2)}, u32[]{:S(2)}) %all-to-all-start.2) | async-done | bytes 524320 | tf_op jit(solution)/shard_map/all_to_all | solution.py:379
  456.1 5.8 %unpack.1 = f32[2,1024,64]{2,1,0:T(8,128)} custom-call(s32[2,1024,1]{2,1,0:T(8,128)} %iota_select_fusion.src_ref, f32[8,64,256]{2,1,0:T(8,128)} %copy-done.4), custom_call_target="tpu_custom_call" | custom-call | tf_op jit(solution)/shard_map/unpack/pallas_call | solution.py:383
  464.2 6.1 %all-gather.8.cloned.1.call-done = f32[16,112,256]{2,1,0:T(8,128)} async-done(((f32[1,112,256]{2,1,0:T(8,128)}), f32[16,112,256]{2,1,0:T(8,128)}) %all-gather.8.cloned.1.call-update) | async-done | bytes 1835024 | tf_op jit(solution)/shard_map/all_gather | solution.py:414
  472.0 15.4 %parent_factor.1 = (f32[256,256]{1,0:T(8,128)}, f32[1,256,256]{2,1,0:T(8,128)}) custom-call(f32[256,256]{1,0:T(8,128)} %slice.79.a_ref), custom_call_target="tpu_custom_call" | custom-call | tf_op jit(solution)/shard_map/parent_factor/pallas_call | solution.py:124
  487.4 12.5 %final.1 = (f32[1536,768]{1,0:T(8,128)}, f32[1536,256]{1,0:T(8,128)}) custom-call(s32[2]{0:T(128)} %pad_add_fusion.1.flag_ref, f32[1,256,256]{2,1,0:T(8,128)} %get-tuple-element.16.w_ref, f32[1536,768]{1,0:T(8,128)} %merge.1.m_ref, f32[1792,256]{1,0:T(8,128)} %bitcast.105, f32[256,768]{1,0:T(8,128)} %bitcast.102), custom_call_target="tpu_custom_call" | custom-call | tf_op jit(solution)/shard_map/final/pallas_call | solution.py:416
  (87 shorter events, 56.7 us)
Async XLA Ops:
  7.2 162.7 %all-gather.10.cloned.1.call-start = ((), (), s32[]{:S(2)}) async-start(), calls=%async_computation.6 | async-start | bytes 4259840 | tf_op jit(solution)/shard_map/all_gather | solution.py:319
  17.3 53.4 %copy-start.7 = (s32[2,1,512]{2,1,0:T(1,128)S(1)}, s32[2,1,512]{2,1,0:T(1,128)}, u32[]{:S(2)}) copy-start(s32[2,1,512]{2,1,0:T(1,128)} %constant_dynamic-slice_fusion.1.pos_ref) | copy-start | bytes 12292
  17.3 12.1 %collective-permute-start = (f32[1024,128]{1,0:T(8,128)S(1)}, f32[1024,128]{1,0:T(8,128)S(1)}, u32[]{:S(2)}, u32[]{:S(2)}) collective-permute-start(f32[1024,128]{1,0:T(8,128)S(1)} %get-tuple-element.41), channel_id=1, source_target_pairs={{0,112},{1,113},{2,114},{3,115},{4,116},{5,117},{6,118},{7,119},{8... | collective-permute-start | bytes 1572872 | tf_op jit(solution)/shard_map/ppermute | solution.py:315
  21.8 12.3 %collective-permute-start.1 = (f32[1024,128]{1,0:T(8,128)S(1)}, f32[1024,128]{1,0:T(8,128)S(1)}, u32[]{:S(2)}, u32[]{:S(2)}) collective-permute-start(f32[1024,128]{1,0:T(8,128)S(1)} %get-tuple-element.40), channel_id=1, source_target_pairs={{0,96},{1,97},{2,98},{3,99},{4,100},{5,101},{6,102},{7,103},{8,104... | collective-permute-start | bytes 1572872 | tf_op jit(solution)/shard_map/ppermute | solution.py:315
  23.1 13.1 %collective-permute-start.2 = (f32[1024,128]{1,0:T(8,128)S(1)}, f32[1024,128]{1,0:T(8,128)}, u32[]{:S(2)}, u32[]{:S(2)}) collective-permute-start(f32[1024,128]{1,0:T(8,128)S(1)} %get-tuple-element.39), channel_id=1, source_target_pairs={{0,80},{1,81},{2,82},{3,83},{4,84},{5,85},{6,86},{7,87},{8,88},{9,... | collective-permute-start | bytes 1572872 | tf_op jit(solution)/shard_map/ppermute | solution.py:315
  25.3 11.5 %collective-permute-start.3 = (f32[1024,128]{1,0:T(8,128)S(1)}, f32[1024,128]{1,0:T(8,128)}, u32[]{:S(2)}, u32[]{:S(2)}) collective-permute-start(f32[1024,128]{1,0:T(8,128)S(1)} %get-tuple-element.38), channel_id=1, source_target_pairs={{0,64},{1,65},{2,66},{3,67},{4,68},{5,69},{6,70},{7,71},{8,72},{9,... | collective-permute-start | bytes 1572872 | tf_op jit(solution)/shard_map/ppermute | solution.py:315
  27.4 15.0 %collective-permute-start.4 = (f32[1024,128]{1,0:T(8,128)S(1)}, f32[1024,128]{1,0:T(8,128)}, u32[]{:S(2)}, u32[]{:S(2)}) collective-permute-start(f32[1024,128]{1,0:T(8,128)S(1)} %get-tuple-element.37), channel_id=1, source_target_pairs={{0,48},{1,49},{2,50},{3,51},{4,52},{5,53},{6,54},{7,55},{8,56},{9,... | collective-permute-start | bytes 1572872 | tf_op jit(solution)/shard_map/ppermute | solution.py:315
  29.4 4.6 copy-start.5
  29.4 18.5 %collective-permute-start.5 = (f32[1024,128]{1,0:T(8,128)S(1)}, f32[1024,128]{1,0:T(8,128)}, u32[]{:S(2)}, u32[]{:S(2)}) collective-permute-start(f32[1024,128]{1,0:T(8,128)S(1)} %get-tuple-element.36), channel_id=1, source_target_pairs={{0,32},{1,33},{2,34},{3,35},{4,36},{5,37},{6,38},{7,39},{8,40},{9,... | collective-permute-start | bytes 1572872 | tf_op jit(solution)/shard_map/ppermute | solution.py:315
  34.1 0.8 copy-start.6
  34.9 13.1 %collective-permute-start.6 = (f32[1024,128]{1,0:T(8,128)S(1)}, f32[1024,128]{1,0:T(8,128)S(1)}, u32[]{:S(2)}, u32[]{:S(2)}) collective-permute-start(f32[1024,128]{1,0:T(8,128)S(1)} %get-tuple-element.35), channel_id=1, source_target_pairs={{0,16},{1,17},{2,18},{3,19},{4,20},{5,21},{6,22},{7,23},{8,24},{9,... | collective-permute-start | bytes 1572872 | tf_op jit(solution)/shard_map/ppermute | solution.py:315
  49.2 29.7 %copy-start.1 = (f32[1024,128]{1,0:T(8,128)}, f32[1024,128]{1,0:T(8,128)S(1)}, u32[]{:S(2)}) copy-start(f32[1024,128]{1,0:T(8,128)S(1)} %fusion.13) | copy-start | bytes 1572868
  70.6 163.4 %all-gather.12.cloned.1.call-start = ((), (), s32[]{:S(2)}) async-start(), calls=%async_computation.7 | async-start | bytes 2293760 | tf_op jit(solution)/shard_map/all_gather | solution.py:346
  140.7 1.9 copy-start
  143.6 127.8 %all-gather.14.cloned.1.call-start = ((), (), s32[]{:S(2)}) async-start(), calls=%async_computation.8 | async-start | bytes 8912896 | tf_op jit(solution)/shard_map/all_gather | solution.py:329
  327.6 6.8 %copy-start.3 = (f32[2,448,896]{2,1,0:T(8,128)S(1)}, f32[2,448,896]{2,1,0:T(8,128)}, u32[]{:S(2)}) copy-start(f32[2,448,896]{2,1,0:T(8,128)} %get-tuple-element.15) | copy-start | bytes 9633796
  330.5 4.0 collective-permute-start.7
  366.4 31.1 %slice-start = ((f32[1536,768]{1,0:T(8,128)}), f32[1536,256]{1,0:T(8,128)S(1)}, s32[]{:S(2)}) async-start(f32[1536,768]{1,0:T(8,128)} %merge.1.m_ref), calls=%async_computation.9 | async-start | bytes 3145728 | tf_op jit(solution)/shard_map/slice | solution.py:412
  366.4 17.6 %all-to-all-start.3 = ((f32[8,32,768]{2,1,0:T(8,128)}), f32[8,32,768]{2,1,0:T(8,128)S(1)}, u32[]{:S(2)}, u32[]{:S(2)}) async-start(f32[8,32,768]{2,1,0:T(8,128)} %bitcast.31), calls=%async_computation.3 | async-start | bytes 1572864 | tf_op jit(solution)/shard_map/all_to_all | solution.py:410
  370.8 99.5 %all-gather.8.cloned.1.call-start = ((), (), s32[]{:S(2)}) async-start(), calls=%async_computation.5 | async-start | bytes 1949696 | tf_op jit(solution)/shard_map/all_gather | solution.py:414
  397.4 31.3 %copy-start.2 = (f32[8,32,768]{2,1,0:T(8,128)}, f32[8,32,768]{2,1,0:T(8,128)S(1)}, u32[]{:S(2)}) copy-start(f32[8,32,768]{2,1,0:T(8,128)S(1)} %all_gather.30) | copy-start | bytes 2359300
  441.2 14.0 %all-to-all-start.2 = ((f32[8,64,256]{2,1,0:T(8,128)}), f32[8,64,256]{2,1,0:T(8,128)S(1)}, u32[]{:S(2)}, u32[]{:S(2)}) async-start(f32[8,64,256]{2,1,0:T(8,128)} %fusion.17), calls=%async_computation.2 | async-start | bytes 1048576 | tf_op jit(solution)/shard_map/all_to_all | solution.py:379
  455.3 0.8 copy-start.4
Sparse Core Ops, SparseCore 0:
  70.7 99.1 all-gather.9
  171.5 26.1 all-gather.11
  200.5 70.9 all-gather.13
  429.6 40.7 all-gather.7

commit v2 on v1

v2 whole, which is shorter than its diff:
```python
from functools import partial

import jax
import jax.numpy as jnp
from jax import lax
from jax.experimental import pallas as pl
from jax.experimental.pallas import tpu as pltpu
from jax.sharding import PartitionSpec as P

F32 = jnp.float32
BF16 = jnp.bfloat16
NB = 256
SB = 64
GROUP = 4
BLK = 512
KEYS = 16
HIGHEST = lax.Precision.HIGHEST
VMEM_LIMIT = 56 << 20


def mm(a, b, ca, cb):
    return lax.dot_general(
        a, b, (((ca,), (cb,)), ((), ())), precision=HIGHEST, preferred_element_type=F32
    )


def mm_bf(a, b, ca, cb):
    return lax.dot_general(a, b, (((ca,), (cb,)), ((), ())), preferred_element_type=F32)


def split2(x):
    hi = x.astype(BF16)
    return hi, (x - hi.astype(F32)).astype(BF16)


def mm3(a, b, ca, cb):
    return mm_bf(a[0], b[0], ca, cb) + (mm_bf(a[0], b[1], ca, cb) + mm_bf(a[1], b[0], ca, cb))


def split3(x):
    hi = x.astype(BF16)
    rest = x - hi.astype(F32)
    mid = rest.astype(BF16)
    low = (rest - mid.astype(F32)).astype(BF16)
    return hi, mid, low


def call(kernel, name, us, **kw):
    return pl.pallas_call(
        kernel,
        name=name,
        cost_estimate=pl.CostEstimate(flops=us * 10**9, transcendentals=0, bytes_accessed=1 << 20),
        compiler_params=pltpu.CompilerParams(vmem_limit_bytes=VMEM_LIMIT),
        **kw,
    )


def factor_small(diag):
    n = SB
    ri = lax.broadcasted_iota(jnp.int32, (n, n), 0)
    ci = lax.broadcasted_iota(jnp.int32, (n, n), 1)
    full = jnp.concatenate([diag, jnp.where(ri == ci, 1.0, 0.0)], axis=1)
    nv = n // 8
    rows = [full[8 * v : 8 * v + 8, :] for v in range(nv)]
    sub = lax.broadcasted_iota(jnp.int32, (8, 2 * n), 0)
    wide = lambda x: jnp.broadcast_to(x, (8, 2 * n))
    pivots = []
    for j0 in range(0, n, GROUP):
        v0 = j0 // 8
        cols = [[wide(rows[v][:, j0 + q : j0 + q + 1]) for v in range(v0, nv)] for q in range(GROUP)]
        at = [(j0 + q) % 8 for q in range(GROUP)]
        lead = [wide(rows[v0][at[q] : at[q] + 1, :]) for q in range(GROUP)]
        for q in range(GROUP):
            inv = 1.0 / wide(cols[q][0][at[q] : at[q] + 1, :])
            pivots.append(inv)
            scaled = lead[q] * inv
            below = [jnp.where(sub > at[q], cols[q][0], 0.0)] + cols[q][1:]
            for t in range(q + 1, GROUP):
                ratio = wide(cols[t][0][at[q] : at[q] + 1, :]) * inv
                weight = wide(cols[q][0][at[t] : at[t] + 1, :])
                cols[t] = [cols[t][i] - below[i] * ratio for i in range(len(below))]
                lead[t] = lead[t] - weight * scaled
            for i in range(len(below)):
                rows[v0 + i] = rows[v0 + i] - below[i] * scaled
    out = []
    for v in range(nv):
        scale = pivots[8 * v]
        for s in range(1, 8):
            scale = jnp.where(sub == s, pivots[8 * v + s], scale)
        out.append(rows[v] * jnp.sqrt(scale))
    return jnp.concatenate(out, axis=0)


def factor_diag(d_ref, w_ref, base):
    ri = lax.broadcasted_iota(jnp.int32, (NB, NB), 0)
    ci = lax.broadcasted_iota(jnp.int32, (NB, NB), 1)
    w_ref[...] = jnp.where(ri == ci, 1.0, 0.0)
    cb = lax.broadcasted_iota(jnp.int32, (SB, NB), 1)
    rb = lax.broadcasted_iota(jnp.int32, (SB, NB), 0)
    block = pl.ds(base, NB)
    for lo in range(0, NB, SB):
        hi = lo + SB
        here = pl.ds(base + lo, SB)
        strip = d_ref[here, block]
        small = factor_small(strip[:, lo:hi])
        both = mm(small[:, SB:], jnp.concatenate([strip, w_ref[lo:hi, :]], axis=1), 1, 0)
        up = jnp.where(cb >= rb + lo, both[:, :NB], 0.0)
        inv = jnp.where(cb <= rb + lo, both[:, NB:], 0.0)
        d_ref[here, block] = up
        w_ref[lo:hi, :] = inv
        if hi < NB:
            update = mm(up[:, hi:], jnp.concatenate([up, inv], axis=1), 0, 0)
            d_ref[pl.ds(base + hi, NB - hi), block] -= update[:, :NB]
            w_ref[hi:, :] -= update[:, NB:]


def factor_all(n, u_ref, w_ref):
    if n == NB:
        factor_diag(u_ref, w_ref.at[0], 0)
        return

    def step(p, carry):
        factor_diag(u_ref, w_ref.at[p], pl.multiple_of(p * NB, NB))
        for lo in range(0, n - NB, NB):

            @pl.when(p == lo // NB)
            def _():
                hi = lo + NB
                right = mm(w_ref[lo // NB], u_ref[lo:hi, hi:], 1, 0)
                u_ref[lo:hi, hi:] = right
                for q in range(hi, n, NB):
                    own = right[:, q - hi : q - hi + NB]
                    u_ref[q : q + NB, q:] -= mm(own, right[:, q - hi :], 0, 0)

        return carry

    lax.fori_loop(0, n // NB, step, 0)
    for lo in range(NB, n, NB):
        u_ref[lo : lo + NB, :lo] = jnp.zeros((NB, lo), F32)


def chol_kernel(n, a_ref, u_ref, w_ref):
    u_ref[...] = a_ref[...]
    factor_all(n, u_ref, w_ref)


def cholesky_upper(a, name):
    n = a.shape[0]
    return call(
        partial(chol_kernel, n),
        name,
        15,
        out_shape=(
            jax.ShapeDtypeStruct((n, n), F32),
            jax.ShapeDtypeStruct((n // NB, NB, NB), F32),
        ),
    )(a)


def one_hot(pos_row, n):
    ids = lax.broadcasted_iota(jnp.int32, (n, pos_row.shape[1]), 0)
    return jnp.where(ids == pos_row, 1.0, 0.0).astype(BF16)


CORNER = (((0, 0), (0, 1), (1, 1), (2, 0), (3, 0)), ((1, 2), (2, 2), (1, 3), (2, 3), (3, 3)))


def pack_kernel(at_ref, pos_ref, f_ref, o_ref):
    on_top = at_ref[0] == 0
    pivot_cols = at_ref[1] < 2
    inner = jnp.logical_not(jnp.logical_or(on_top, pivot_cols))

    for h in range(2):

        @pl.when(jnp.logical_and(on_top, at_ref[1] == h))
        def _():
            for y in range(4):
                for p in range(KEYS):
                    for t in range(5):
                        at = (p * 5 + t) * 8
                        rb, cb = CORNER[h][at // 128]
                        row = rb * NB + y * 64 + at % 64
                        lane = (cb - 2 * h) * NB + (at % 128) // 64 * 128
                        o_ref[y, 0, p, t * 8 : t * 8 + 8, :] = f_ref[
                            0, row : row + 8, lane : lane + 128
                        ]

    @pl.when(jnp.logical_and(on_top, jnp.logical_not(pivot_cols)))
    def _():
        place = one_hot(pos_ref[0, 2:3, :], BLK)
        out = sum(mm_bf(part, place, 1, 1) for part in split3(f_ref[0]))
        for y in range(4):
            for p in range(KEYS):
                o_ref[y, 0, p] = out[p * 64 : (p + 1) * 64, y * 128 : (y + 1) * 128]

    def store(b, total):
        for y in range(4):
            for p in range(KEYS):
                o_ref[y, 0, p, b * 32 : (b + 1) * 32, :] = total[
                    p * 32 : (p + 1) * 32, y * 128 : (y + 1) * 128
                ]

    def by_row(b):
        place_row = one_hot(pos_ref[0, b : b + 1, :], BLK)
        return [mm_bf(place_row, part, 1, 0) for part in split3(f_ref[0, b * BLK : (b + 1) * BLK, :])]

    @pl.when(jnp.logical_and(jnp.logical_not(on_top), pivot_cols))
    def _():
        for b in range(2):
            store(b, sum(by_row(b)))

    @pl.when(inner)
    def _():
        place_col = one_hot(pos_ref[0, 2:3, :], BLK)
        for b in range(2):
            store(b, sum(mm_bf(place_col, row.astype(BF16), 1, 1) for row in by_row(b)))


def chol_gathered_kernel(at_ref, a_ref, u_ref, w_ref):
    for yy in range(4):
        back = (at_ref[0] - yy) & 3
        for pc in range(KEYS):
            for t in range(5):
                at = (pc * 5 + t) * 8
                blk, q, i = at // 128, (at % 128) // 64, at % 64
                for h in range(2):
                    rb, cb = CORNER[h][blk]
                    row = rb * NB + yy * 64 + i
                    lane = cb * NB + q * 128
                    u_ref[row : row + 8, lane : lane + 128] = a_ref[pc, back, h, t * 8 : t * 8 + 8]
    for cb in (2, 3):
        u_ref[0:NB, cb * NB : (cb + 1) * NB] = u_ref[cb * NB : (cb + 1) * NB, 0:NB].T
    factor_all(u_ref.shape[0], u_ref, w_ref)


def pair(ref, rows, cols):
    return ref[0, rows, cols], ref[1, rows, cols]


def put(ref, rows, cols, value):
    ref[0, rows, cols], ref[1, rows, cols] = split2(value)


def rows_kernel(at_ref, u_ref, w_ref, x_ref, rxs_ref, o_ref, rx_ref, low_ref, inv_ref):
    step = pl.program_id(0)
    panels = u_ref.shape[0] // NB
    every = slice(None)
    strip = pl.ds(pl.multiple_of(at_ref[1] * 64, 64), 64)

    @pl.when(step == 0)
    def _():
        for p in range(panels):
            now, done = slice(p * NB, (p + 1) * NB), slice(0, p * NB)
            put(inv_ref, now, every, w_ref[p])
            if p:
                put(low_ref, now, done, u_ref[done, now].T)
        for yy in range(4):

            @pl.when(at_ref[0] == yy)
            def _():
                o_ref[0] = u_ref[strip, yy * NB : (yy + 1) * NB]

    @pl.when(step > 0)
    def _():
        for p in range(panels):
            now, done = slice(p * NB, (p + 1) * NB), slice(0, p * NB)
            cur = jnp.concatenate(
                [x_ref[4 * p : 4 * p + 4, t].reshape(NB, 128) for t in range(2)], axis=1
            )
            if p:
                cur = cur - mm3(pair(low_ref, now, done), pair(rxs_ref, done, every), 1, 0)
            cur = mm3(pair(inv_ref, now, every), split2(cur), 1, 0)
            rx_ref[now, :] = cur
            put(rxs_ref, now, every, cur)
        o_ref[0] = rx_ref[strip, :]


def schur_kernel(at_ref, u_ref, w_ref, y_ref, rxs_ref, c_ref, s_ref, ry_ref):
    step = pl.program_id(0)
    panels = u_ref.shape[0] // NB
    every = slice(None)

    @pl.when(step == 0)
    def _():
        for p in range(panels):
            now, done = slice(p * NB, (p + 1) * NB), slice(0, p * NB)
            cur = jnp.concatenate(
                [
                    y_ref[(at_ref[0] - (2 * p + t)) & 3, :, (2 * p + t) // 4].reshape(448, 128)
                    for t in range(2)
                ],
                axis=1,
            )
            if p:
                cur = cur - mm3(pair(ry_ref, every, done), split2(u_ref[done, now]), 1, 0)
            put(ry_ref, every, now, mm3(split2(cur), split2(w_ref[p]), 1, 1))

    @pl.when(step > 0)
    def _():
        prod = mm3(pair(ry_ref, every, every), pair(rxs_ref, every, every), 1, 0)
        c0 = c_ref[0, 2:, 0:32, :].reshape(448, 128) - prod[:, :128]
        c1 = c_ref[0, 2:, 32:64, :].reshape(448, 128) - prod[:, 128:]
        lane = lax.broadcasted_iota(jnp.int32, (448, 128), 1)
        s_ref[0] = jnp.where(lane < 64, c0, pltpu.roll(c1, 64, 1))
        s_ref[1] = jnp.where(lane < 64, pltpu.roll(c0, 64, 1), c1)


def unpack_kernel(src_ref, r_ref, o_ref):
    for k in range(2):
        wide = jnp.concatenate([r_ref[2 * yy + k] for yy in range(4)], axis=1)
        place = one_hot_rows(src_ref[k], 1024)
        o_ref[k] = sum(mm_bf(place, part, 1, 1) for part in split3(wide))


def one_hot_rows(src_col, n):
    ids = lax.broadcasted_iota(jnp.int32, (src_col.shape[0], n), 1)
    return jnp.where(ids == src_col, 1.0, 0.0).astype(BF16)


def merge_kernel(core_ref, tx_ref, ty_ref, s_ref, g_ref, p_ref, o_ref, part_ref, ey_ref):
    tile = pl.program_id(0)

    @pl.when(tile == 0)
    def _():
        for k in range(2):
            ey_ref[k] = one_hot(ty_ref[k], 768)
        core = core_ref[0]
        part_ref[core, 0], part_ref[core, 1] = split2(s_ref[0])
        part_ref[1 - core, 0], part_ref[1 - core, 1] = split2(g_ref[...])

    acc = p_ref[...]
    for k in range(2):
        ex = one_hot(tx_ref[k] - tile * NB, NB)
        for i in range(2):
            half = mm_bf(ex, part_ref[k, i], 1, 1)
            acc = acc + mm_bf(half.astype(BF16), ey_ref[k], 1, 1)
    o_ref[...] = acc


def final_kernel(flag_ref, w_ref, m_ref, row_ref, col_ref, o_ref, f_ref, rc_ref):
    tile = pl.program_id(0)
    inv = split2(w_ref[0])

    @pl.when(tile == 0)
    def _():
        rc_ref[0], rc_ref[1] = split2(mm3(inv, split2(col_ref[...]), 1, 0))

    rows = mm3(split2(row_ref[...]), inv, 1, 1)
    f_ref[...] = rows
    out = m_ref[...] - mm3(split2(rows), (rc_ref[0], rc_ref[1]), 1, 0)
    lane = lax.broadcasted_iota(jnp.int32, out.shape, 1)
    keep_row = jnp.logical_or(flag_ref[0] != 0, tile > 0)
    keep = jnp.logical_and(keep_row, jnp.logical_or(flag_ref[1] != 0, lane >= NB))
    o_ref[...] = jnp.where(keep, out, 0.0)


def smem():
    return pl.BlockSpec(memory_space=pltpu.SMEM)


def whole(shape):
    return pl.BlockSpec(shape, lambda *_: (0,) * len(shape))


def local(child_fronts, parent_front, child_map):
    r = lax.axis_index("row")
    c = lax.axis_index("col")
    core = r % 2
    y = r // 2
    nblk = child_map.shape[1] // BLK

    maps = child_map.reshape(2 * nblk, BLK)
    keys = maps // 768
    hot = (keys[:, :, None] == jnp.arange(KEYS, dtype=jnp.int32)).astype(BF16)
    lower = (jnp.arange(BLK)[:, None] >= jnp.arange(BLK)[None, :]).astype(BF16)
    counts = jnp.einsum("ef,bfk->bek", lower, hot, preferred_element_type=F32)
    rank = jnp.sum(counts * hot.astype(F32), axis=2).astype(jnp.int32) - 1
    pos = (keys * 32 + rank).reshape(2, nblk, BLK)
    maps = maps.reshape(2, nblk, BLK)

    pos_c = lax.dynamic_slice_in_dim(pos, jnp.maximum(c - 2, 0), 1, axis=1)
    pos_r = lax.dynamic_slice_in_dim(pos, jnp.maximum(2 * r - 2, 0), 2, axis=1)

    shifts = [[(i, (i + 2 * s) % 8) for i in range(8)] for s in (1, 2, 3)]

    def gather_y(x):
        return jnp.stack([x] + [lax.ppermute(x, "row", pairs) for pairs in shifts])

    def swap(x, axes):
        return lax.all_to_all(x, axes, split_axis=0, concat_axis=0, tiled=True)

    def repeat(x, axes, parts):
        x = lax.optimization_barrier(x)
        return swap(jnp.broadcast_to(x[None], (parts, *x.shape)), axes)

    at = jnp.stack([y, c])
    packed = call(
        pack_kernel,
        "pack",
        8,
        grid=(2,),
        in_specs=[
            smem(),
            pl.BlockSpec((1, 3, BLK), lambda k: (k, 0, 0)),
            pl.BlockSpec((1, 1024, BLK), lambda k: (k, 0, 0)),
        ],
        out_specs=pl.BlockSpec((4, 1, KEYS, 64, 128), lambda k: (0, k, 0, 0, 0)),
        out_shape=jax.ShapeDtypeStruct((4, 2, KEYS, 64, 128), F32),
    )(jnp.stack([r, c]), jnp.concatenate([pos_r, pos_c], axis=1), child_fronts)
    arrived = swap(packed.reshape(8 * KEYS, 64, 128), ("row", "col")).reshape(8, KEYS, 64, 128)
    spread = gather_y(arrived[0, :2, :40])
    pieces = lax.all_gather(spread, "col")
    own_x, _ = lax.optimization_barrier((arrived[0, 2:], spread))
    panel_x = lax.all_gather(own_x, "col")
    upper, inverses = call(
        chol_gathered_kernel,
        "child_factor",
        64,
        in_specs=[smem(), whole((KEYS, 4, 2, 40, 128))],
        out_shape=(
            jax.ShapeDtypeStruct((1024, 1024), F32),
            jax.ShapeDtypeStruct((4, NB, NB), F32),
        ),
    )(at, pieces)
    mine_y = arrived[1:, :2]
    shifted_y = [lax.ppermute(mine_y, "row", pairs) for pairs in shifts]

    factor_x, outgoing = call(
        rows_kernel,
        "rows",
        20,
        grid=(8,),
        in_specs=[
            smem(),
            whole((1024, 1024)),
            whole((4, NB, NB)),
            pl.BlockSpec((KEYS, 2, 64, 128), lambda g: (0, jnp.maximum(g, 1) - 1, 0, 0)),
        ],
        out_specs=(
            pl.BlockSpec((2, 1024, NB), lambda g: (0, 0, jnp.maximum(g, 1) - 1)),
            pl.BlockSpec((1, 64, NB), lambda g: (g, 0, 0)),
        ),
        out_shape=(
            jax.ShapeDtypeStruct((2, 1024, 1792), BF16),
            jax.ShapeDtypeStruct((8, 64, NB), F32),
        ),
        scratch_shapes=[
            pltpu.VMEM((1024, NB), F32),
            pltpu.VMEM((2, 1024, 1024), BF16),
            pltpu.VMEM((2, 1024, NB), BF16),
        ],
    )(at, upper, inverses, panel_x)
    factor_x, *shifted_y = lax.optimization_barrier((factor_x, *shifted_y))
    panel_y = jnp.stack([mine_y, *shifted_y])
    landed = swap(outgoing, "row")
    schur = call(
        schur_kernel,
        "schur",
        18,
        grid=(8,),
        in_specs=[
            smem(),
            whole((1024, 1024)),
            whole((4, NB, NB)),
            whole((4, 7, 2, 64, 128)),
            pl.BlockSpec((2, 1024, NB), lambda g: (0, 0, jnp.maximum(g, 1) - 1)),
            pl.BlockSpec((1, KEYS, 64, 128), lambda g: (jnp.maximum(g, 1), 0, 0, 0)),
        ],
        out_specs=pl.BlockSpec((2, 448, 128), lambda g: (0, 0, jnp.maximum(g, 1) - 1)),
        out_shape=jax.ShapeDtypeStruct((2, 448, 896), F32),
        scratch_shapes=[pltpu.VMEM((2, 448, 1024), BF16)],
    )(at, upper, inverses, panel_y, factor_x, arrived)

    got = lax.ppermute(
        lax.dynamic_index_in_dim(schur, 1 - core, 0, keepdims=False),
        "row",
        [(i, i ^ 1) for i in range(8)],
    )

    spot = (pos_r // 128) * NB + jnp.arange(2, dtype=jnp.int32)[None, :, None] * 128 + pos_r % 128
    natural = jnp.broadcast_to(jnp.arange(1024, dtype=jnp.int32), (2, 1024))
    spot = jnp.where(r == 0, natural, spot.reshape(2, 1024))
    def sorted_maps(start, count):
        ids = start + jnp.arange(count, dtype=jnp.int32)
        return jnp.sum(
            jnp.where(pos[:, :, :, None] == ids, maps[:, :, :, None], 0), axis=2, dtype=jnp.int32
        )

    to_rows = sorted_maps(r * 64, 64).reshape(2, 1, 896) - r * 1536
    to_cols = sorted_maps(c * 32, 32).reshape(2, 1, 448) - c * 768
    merged = pl.pallas_call(
        merge_kernel,
        name="merge",
        cost_estimate=pl.CostEstimate(flops=19 * 10**9, transcendentals=0, bytes_accessed=1 << 20),
        compiler_params=pltpu.CompilerParams(vmem_limit_bytes=VMEM_LIMIT),
        grid_spec=pltpu.PrefetchScalarGridSpec(
            num_scalar_prefetch=1,
            grid=(6,),
            in_specs=[
                whole((2, 1, 896)),
                whole((2, 1, 448)),
                pl.BlockSpec((1, 448, 896), lambda t, which: (which[0], 0, 0)),
                whole((448, 896)),
                pl.BlockSpec((NB, 768), lambda t, which: (t, 0)),
            ],
            out_specs=pl.BlockSpec((NB, 768), lambda t, which: (t, 0)),
            scratch_shapes=[pltpu.VMEM((2, 2, 448, 896), BF16), pltpu.VMEM((2, 768, 448), BF16)],
        ),
        out_shape=jax.ShapeDtypeStruct((1536, 768), F32),
    )(core[None], to_rows, to_cols, schur, got, parent_front)
    merged, landed = lax.optimization_barrier((merged, landed))
    child_factor = call(
        unpack_kernel, "unpack", 6, out_shape=jax.ShapeDtypeStruct((2, 1024, 64), F32)
    )(spot[:, :, None], landed)

    top = repeat(swap(merged[:NB].reshape(8, 32, 768), "row")[0], "row", 8).reshape(NB, 768)
    side = jnp.concatenate([merged[:, :NB], top[:, :NB]]).reshape(KEYS, 112, NB)
    side, child_factor = lax.optimization_barrier((swap(side, "col")[0], child_factor))
    left = repeat(side, "col", KEYS).reshape(1792, NB)
    _, parent_inverse = cholesky_upper(left[1536:], "parent_factor")
    schur_out, rows_out = call(
        final_kernel,
        "final",
        10,
        grid=(6,),
        in_specs=[
            smem(),
            whole((1, NB, NB)),
            pl.BlockSpec((NB, 768), lambda t: (t, 0)),
            pl.BlockSpec((NB, NB), lambda t: (t, 0)),
            whole((NB, 768)),
        ],
        out_specs=(
            pl.BlockSpec((NB, 768), lambda t: (t, 0)),
            pl.BlockSpec((NB, NB), lambda t: (t, 0)),
        ),
        out_shape=(
            jax.ShapeDtypeStruct((1536, 768), F32),
            jax.ShapeDtypeStruct((1536, NB), F32),
        ),
        scratch_shapes=[pltpu.VMEM((2, NB, 768), BF16)],
    )(jnp.stack([r, c]), parent_inverse, merged, left, top)
    parent_factor = lax.dynamic_slice_in_dim(rows_out, c * 16, 16, axis=1)
    return child_factor, parent_factor, schur_out


def solution(mesh):
    return jax.shard_map(
        local,
        mesh=mesh,
        in_specs=(P(None, "row", "col"), P("row", "col"), P()),
        out_specs=(P(None, "row", "col"), P("row", "col"), P("row", "col")),
        check_vma=False,
    )
```

time: 517 us -> 424 us (0.82)
  blocking collectives: 127 us -> 86.4 us
  Pallas kernels: 192 us -> 159 us
  local copies, waits for them, and re-layouts: 34.9 us -> 17.6 us
    all_to_all x2 -> x4, waiting for transfers between devices: 20.8 us -> 58.6 us  [swap(): return lax.all_to_all(x, axes, split_axis=0, concat_axis=0, tiled=True)]
    pallas_call x8, Pallas kernels: 192 us -> 159 us  [the longest x1 63.9 us: local(): call(chol_gathered_kernel, 'child_factor', 64, in_specs=[smem(), whole((K...]
    all_gather x4 -> x2, waiting for transfers between devices: 69.1 us -> 39.5 us  [the longest x1 35.2 us: local(): pieces = lax.all_gather(spread, 'col')]
    all_to_all x3 -> x2, blocking collectives: 114 us -> 86.4 us  [swap(): return lax.all_to_all(x, axes, split_axis=0, concat_axis=0, tiled=True)]
    all_gather x1 -> x0, blocking collectives: 13.5 us -> none  [local(): top = lax.all_gather(down[0], 'row').reshape(NB, 768)]
    unnamed x25 -> x12, local copies, waits for them, and re-layouts: 17.1 us -> 3.98 us
    ppermute x8 -> x7, waiting for transfers between devices: 15.4 us -> 4.46 us  [the longest x3 4.45 us: gather_y(): return jnp.stack([x] + [lax.ppermute(x, 'row', pairs) for pairs in shifts])]
    all_to_all x2 -> x4, starting transfers between devices: 8.16 us -> 17.3 us  [swap(): return lax.all_to_all(x, axes, split_axis=0, concat_axis=0, tiled=True)]
  transfers between devices with their start and end apart: 14 -> 13, of which waited for: 10 -> 8; matrix products, arithmetic and copies ran while one was open for 4% -> 2% of each run, Pallas kernels for 15% -> 27%
where the time goes in v2:
time: 424 us; the launch traced here: 416 us
  Pallas kernels  159 us (38%)
  waiting for transfers between devices  103 us (24%)
  blocking collectives  86.4 us (20%)
  starting transfers between devices  25.3 us (6%)
  local copies, waits for them, and re-layouts  17.6 us (4%)
  between operations  14.8 us (3%)
  other arithmetic  9.68 us (2%)
    all_to_all x2, blocking collectives, swap(): return lax.all_to_all(x, axes, split_axis=0, concat_axis=0, tiled=True)  86.4 us
    pallas_call x1, Pallas kernels, local(): call(chol_gathered_kernel, 'child_factor', 64, in_specs=[smem(), whole((K...  63.9 us
    all_to_all x4, waiting for transfers between devices, swap(): return lax.all_to_all(x, axes, split_axis=0, concat_axis=0, tiled=True)  58.6 us
    all_gather x1, waiting for transfers between devices, local(): pieces = lax.all_gather(spread, 'col')  35.2 us
    pallas_call x1, Pallas kernels, local(): call(rows_kernel, 'rows', 20, grid=(8,), in_specs=[smem(), whole((1024, 1...  24.3 us
    pallas_call x1, Pallas kernels, local(): pl.pallas_call(merge_kernel, name='merge', cost_estimate=pl.CostEstimate(...  19.4 us
    all_to_all x4, starting transfers between devices, swap(): return lax.all_to_all(x, axes, split_axis=0, concat_axis=0, tiled=True)  17.3 us
    pallas_call x1, Pallas kernels, local(): call(schur_kernel, 'schur', 18, grid=(8,), in_specs=[smem(), whole((1024,...  16.6 us
  transfers between devices with their start and end apart: 13, of which 8 were waited for; matrix products, arithmetic and copies ran while one was open for 2% of the time, Pallas kernels for 27%

profile of v2, /device:TPU:0, one launch (start us, length us, event | category | flops | bytes accessed | tf_op | source)
XLA Modules:
  0.0 415.9 jit_solution(5348946332859636037)
XLA Ops:
  12.0 3.7 pack.1
  15.8 68.5 %all_to_all.30 = f32[128,64,128]{2,1,0:T(8,128)S(1)} all-to-all(f32[128,64,128]{2,1,0:T(8,128)} %bitcast.44), channel_id=1, replica_groups=mesh['row'=8,'col'=16] {'row','col'}, dimensions={0} | all-to-all | bytes 8388608 | tf_op jit(solution)/shard_map/all_to_all | solution.py:390
  84.3 2.0 copy-done
  86.3 1.9 collective-permute-start.2
  90.3 3.4 collective-permute-done.1
  98.7 2.1 collective-permute-start.4
  100.9 2.1 collective-permute-start.5
  102.9 35.2 %all-gather.5.cloned.1.call-done = f32[64,2,40,128]{3,2,1,0:T(8,128)} async-done(((f32[4,2,40,128]{3,2,1,0:T(8,128)}), f32[64,2,40,128]{3,2,1,0:T(8,128)}) %all-gather.5.cloned.1.call-update) | async-done | bytes 2621456 | tf_op jit(solution)/shard_map/all_gather | solution.py:412
  138.1 63.9 %child_factor.1 = (f32[1024,1024]{1,0:T(8,128)}, f32[4,256,256]{2,1,0:T(8,128)}) custom-call(s32[2]{0:T(128)} %pad_add_fusion.1.at_ref, f32[16,4,2,40,128]{4,3,2,1,0:T(8,128)} %bitcast.56), custom_call_target="tpu_custom_call" | custom-call | flops 64000000000 | bytes 1048576 | tf_op jit(solution)/shard_map/child_factor/pallas_call | solution.py:415
  202.0 4.3 %all-gather.7.cloned.1.call-done = f32[224,64,128]{2,1,0:T(8,128)} async-done(((f32[14,64,128]{2,1,0:T(8,128)}), f32[224,64,128]{2,1,0:T(8,128)}) %all-gather.7.cloned.1.call-update) | async-done | bytes 7340048 | tf_op jit(solution)/shard_map/all_gather | solution.py:414
  206.3 24.3 %rows.1 = (bf16[2,1024,1792]{2,1,0:T(8,128)(2,1)}, f32[8,64,256]{2,1,0:T(8,128)}) custom-call(s32[2]{0:T(128)} %pad_add_fusion.1.at_ref, f32[1024,1024]{1,0:T(8,128)} %get-tuple-element.19.u_ref, f32[4,256,256]{2,1,0:T(8,128)} %get-tuple-element.20.w_ref, f32[16,14,64,128]{3,2,1,0:T(8,128)} %bitcast.55), custom_call_target="tpu_custom_call" | custom-call | flops 20000000000 | bytes 1048576 | tf_op jit(solution)/shard_map/rows/pallas_call | solution.py:428
  232.0 16.6 %schur.1.s_ref = f32[2,448,896]{2,1,0:T(8,128)} custom-call(s32[2]{0:T(128)} %pad_add_fusion.1.at_ref, f32[1024,1024]{1,0:T(8,128)} %get-tuple-element.19.u_ref, f32[4,256,256]{2,1,0:T(8,128)} %get-tuple-element.20.w_ref, f32[4,7,2,64,128]{4,3,2,1,0:T(8,128)} %pad_maximum_fusion.y_ref, bf16[2,1024,1792]{2,1,0:T(8,128)(2,1)} %get-tuple-element.26.rxs_ref, ...), custom_call_target="tpu_custom_call" | custom-call | flops 17999998976 | bytes 1048576 | tf_op jit(solution)/shard_map/schur/pallas_call | solution.py:456
  252.9 4.4 %all-to-all-start.1 = ((f32[8,64,256]{2,1,0:T(8,128)}), f32[8,64,256]{2,1,0:T(8,128)S(1)}, u32[]{:S(2)}, u32[]{:S(2)}) async-start(f32[8,64,256]{2,1,0:T(8,128)} %get-tuple-element.27), calls=%async_computation.1 | async-start | bytes 1048576 | tf_op jit(solution)/shard_map/all_to_all | solution.py:390
  257.3 19.4 %merge.1.m_ref = f32[1536,768]{1,0:T(8,128)} custom-call(s32[1]{0:T(128)} %bitcast.core_ref, s32[2,1,896]{2,1,0:T(1,128)} %sub.64.tx_ref, s32[2,1,448]{2,1,0:T(1,128)} %sub.65.ty_ref, f32[2,448,896]{2,1,0:T(8,128)} %schur.1.s_ref, f32[448,896]{1,0:T(8,128)} %collective-permute-done.6.g_ref, f32[1536,768]{1,0:T(8,128)} %p_ref.1), custom_call_target="tpu_custom_call" | custom-call | flops 19000000512 | bytes 1048576 | tf_op jit(solution)/shard_map/merge/pallas_call | solution.py:491
  278.0 17.8 %all_to_all.31 = f32[8,32,768]{2,1,0:T(8,128)S(1)} all-to-all(f32[8,32,768]{2,1,0:T(8,128)S(1)} %bitcast.43), channel_id=1, replica_groups=mesh['row'=8,'col'=16] {'row'}, dimensions={0} | all-to-all | bytes 1572864 | tf_op jit(solution)/shard_map/all_to_all | solution.py:390
  296.8 3.5 all-to-all-start.3
  300.4 13.1 %all-to-all-done.3 = f32[8,32,768]{2,1,0:T(8,128)S(1)} async-done(((f32[8,32,768]{2,1,0:T(8,128)}), f32[8,32,768]{2,1,0:T(8,128)S(1)}, u32[]{:S(2)}, u32[]{:S(2)}) %all-to-all-start.3) | async-done | bytes 786464 | tf_op jit(solution)/shard_map/all_to_all | solution.py:390
  314.9 5.5 %all-to-all-start.4 = ((f32[16,112,256]{2,1,0:T(8,128)}), f32[16,112,256]{2,1,0:T(8,128)S(1)}, u32[]{:S(2)}, u32[]{:S(2)}) async-start(f32[16,112,256]{2,1,0:T(8,128)} %bitcast.23), calls=%async_computation.4 | async-start | bytes 3670016 | tf_op jit(solution)/shard_map/all_to_all | solution.py:390
  322.5 5.8 %unpack.1 = f32[2,1024,64]{2,1,0:T(8,128)} custom-call(s32[2,1024,1]{2,1,0:T(8,128)} %iota_select_fusion.src_ref, f32[8,64,256]{2,1,0:T(8,128)} %copy-done.4), custom_call_target="tpu_custom_call" | custom-call | flops 6000000000 | bytes 1048576 | tf_op jit(solution)/shard_map/unpack/pallas_call | solution.py:512
  328.3 19.7 %all-to-all-done.4 = f32[16,112,256]{2,1,0:T(8,128)S(1)} async-done(((f32[16,112,256]{2,1,0:T(8,128)}), f32[16,112,256]{2,1,0:T(8,128)S(1)}, u32[]{:S(2)}, u32[]{:S(2)}) %all-to-all-start.4) | async-done | bytes 1835040 | tf_op jit(solution)/shard_map/all_to_all | solution.py:390
  349.4 3.8 all-to-all-start.5
  354.4 25.9 %all-to-all-done.5 = f32[16,112,256]{2,1,0:T(8,128)S(1)} async-done(((f32[16,112,256]{2,1,0:T(8,128)}), f32[16,112,256]{2,1,0:T(8,128)S(1)}, u32[]{:S(2)}, u32[]{:S(2)}) %all-to-all-start.5) | async-done | bytes 1835040 | tf_op jit(solution)/shard_map/all_to_all | solution.py:390
  381.0 15.5 %parent_factor.1 = (f32[256,256]{1,0:T(8,128)}, f32[1,256,256]{2,1,0:T(8,128)}) custom-call(f32[256,256]{1,0:T(8,128)} %slice.42.a_ref), custom_call_target="tpu_custom_call" | custom-call | flops 15000000512 | bytes 1048576 | tf_op jit(solution)/shard_map/parent_factor/pallas_call | solution.py:149
  396.5 9.9 %final.1 = (f32[1536,768]{1,0:T(8,128)}, f32[1536,256]{1,0:T(8,128)}) custom-call(s32[2]{0:T(128)} %pad_add_fusion.2.at_ref.flag_ref, f32[1,256,256]{2,1,0:T(8,128)} %get-tuple-element.32.w_ref, f32[1536,768]{1,0:T(8,128)} %merge.1.m_ref, f32[1792,256]{1,0:T(8,128)} %bitcast.46, f32[256,768]{1,0:T(8,128)} %bitcast.48), custom_call_target="tpu_custom_call" | custom-call | flops 10000000000 | bytes 1048576 | tf_op jit(solution)/shard_map/final/pallas_call | solution.py:521
  (70 shorter events, 28.8 us)
Async XLA Ops:
  7.2 131.0 %all-gather.5.cloned.1.call-start = ((), (), s32[]{:S(2)}) async-start(), calls=%async_computation.6 | async-start | bytes 2785280 | tf_op jit(solution)/shard_map/all_gather | solution.py:412
  84.3 2.0 copy-start
  86.3 4.0 collective-permute-start.2
  88.2 5.5 %collective-permute-start.1 = (f32[2,40,128]{2,1,0:T(8,128)S(1)}, f32[2,40,128]{2,1,0:T(8,128)S(1)}, u32[]{:S(2)}, u32[]{:S(2)}) collective-permute-start(f32[2,40,128]{2,1,0:T(8,128)S(1)} %get-tuple-element.52), channel_id=1, source_target_pairs={{0,64},{16,80},{32,96},{48,112},{64,0},{80,16},{96,32},{112,48},{1... | collective-permute-start | bytes 122888 | tf_op jit(solution)/shard_map/ppermute | solution.py:387
  89.1 5.2 %collective-permute-start = (f32[2,40,128]{2,1,0:T(8,128)S(1)}, f32[2,40,128]{2,1,0:T(8,128)S(1)}, u32[]{:S(2)}, u32[]{:S(2)}) collective-permute-start(f32[2,40,128]{2,1,0:T(8,128)S(1)} %get-tuple-element.52), channel_id=1, source_target_pairs={{0,32},{16,48},{32,64},{48,80},{64,96},{80,112},{96,0},{112,16},{1... | collective-permute-start | bytes 122888 | tf_op jit(solution)/shard_map/ppermute | solution.py:387
  95.0 111.3 %all-gather.7.cloned.1.call-start = ((), (), s32[]{:S(2)}) async-start(), calls=%async_computation.7 | async-start | bytes 7798784 | tf_op jit(solution)/shard_map/all_gather | solution.py:414
  98.7 131.9 %collective-permute-start.3 = (f32[7,2,64,128]{3,2,1,0:T(8,128)S(1)}, f32[7,2,64,128]{3,2,1,0:T(8,128)S(1)}, u32[]{:S(2)}, u32[]{:S(2)}) collective-permute-start(f32[7,2,64,128]{3,2,1,0:T(8,128)S(1)} %get-tuple-element.50), channel_id=1, source_target_pairs={{0,32},{16,48},{32,64},{48,80},{64,96},{80,112},{96,0},{112,16},{1... | collective-permute-start | bytes 1376264 | tf_op jit(solution)/shard_map/ppermute | solution.py:426
  98.7 131.8 %collective-permute-start.4 = (f32[7,2,64,128]{3,2,1,0:T(8,128)S(1)}, f32[7,2,64,128]{3,2,1,0:T(8,128)S(1)}, u32[]{:S(2)}, u32[]{:S(2)}) collective-permute-start(f32[7,2,64,128]{3,2,1,0:T(8,128)S(1)} %get-tuple-element.50), channel_id=1, source_target_pairs={{0,64},{16,80},{32,96},{48,112},{64,0},{80,16},{96,32},{112,48},{1... | collective-permute-start | bytes 1376264 | tf_op jit(solution)/shard_map/ppermute | solution.py:426
  100.9 129.7 %collective-permute-start.5 = (f32[7,2,64,128]{3,2,1,0:T(8,128)S(1)}, f32[7,2,64,128]{3,2,1,0:T(8,128)S(1)}, u32[]{:S(2)}, u32[]{:S(2)}) collective-permute-start(f32[7,2,64,128]{3,2,1,0:T(8,128)S(1)} %get-tuple-element.50), channel_id=1, source_target_pairs={{0,96},{16,112},{32,0},{48,16},{64,32},{80,48},{96,64},{112,80},{1... | collective-permute-start | bytes 1376264 | tf_op jit(solution)/shard_map/ppermute | solution.py:426
  250.1 7.1 %collective-permute-start.6 = (f32[448,896]{1,0:T(8,128)S(1)}, f32[448,896]{1,0:T(8,128)}, u32[]{:S(2)}, u32[]{:S(2)}) collective-permute-start(f32[448,896]{1,0:T(8,128)S(1)} %dynamic-slice_bitcast_fusion), channel_id=1, source_target_pairs={{0,16},{16,0},{32,48},{48,32},{64,80},{80,64},{96,112},{112,96},{1... | collective-permute-start | bytes 4816904 | tf_op jit(solution)/shard_map/ppermute | solution.py:474
  252.9 23.8 %all-to-all-start.1 = ((f32[8,64,256]{2,1,0:T(8,128)}), f32[8,64,256]{2,1,0:T(8,128)S(1)}, u32[]{:S(2)}, u32[]{:S(2)}) async-start(f32[8,64,256]{2,1,0:T(8,128)} %get-tuple-element.27), calls=%async_computation.1 | async-start | bytes 1048576 | tf_op jit(solution)/shard_map/all_to_all | solution.py:390
  276.7 1.3 slice-start
  276.7 20.1 %copy-start.4 = (f32[8,64,256]{2,1,0:T(8,128)}, f32[8,64,256]{2,1,0:T(8,128)S(1)}, u32[]{:S(2)}) copy-start(f32[8,64,256]{2,1,0:T(8,128)S(1)} %all-to-all-done.1.r_ref) | copy-start | bytes 1572868
  296.8 16.6 %all-to-all-start.3 = ((f32[8,32,768]{2,1,0:T(8,128)}), f32[8,32,768]{2,1,0:T(8,128)S(1)}, u32[]{:S(2)}, u32[]{:S(2)}) async-start(f32[8,32,768]{2,1,0:T(8,128)} %broadcast_in_dim.55), calls=%async_computation.3 | async-start | bytes 1572864 | tf_op jit(solution)/shard_map/all_to_all | solution.py:390
  300.4 13.1 %slice-start.1 = ((f32[1536,768]{1,0:T(8,128)}), f32[1536,256]{1,0:T(8,128)S(1)}, s32[]{:S(2)}) async-start(f32[1536,768]{1,0:T(8,128)} %merge.1.m_ref), calls=%async_computation.9 | async-start | bytes 3145728 | tf_op jit(solution)/shard_map/slice | solution.py:517
  313.4 1.5 copy-start.2
  314.9 33.1 %all-to-all-start.4 = ((f32[16,112,256]{2,1,0:T(8,128)}), f32[16,112,256]{2,1,0:T(8,128)S(1)}, u32[]{:S(2)}, u32[]{:S(2)}) async-start(f32[16,112,256]{2,1,0:T(8,128)} %bitcast.23), calls=%async_computation.4 | async-start | bytes 3670016 | tf_op jit(solution)/shard_map/all_to_all | solution.py:390
  349.4 3.9 copy-start.3
  349.4 30.8 %all-to-all-start.5 = ((f32[16,112,256]{2,1,0:T(8,128)}), f32[16,112,256]{2,1,0:T(8,128)S(1)}, u32[]{:S(2)}, u32[]{:S(2)}) async-start(f32[16,112,256]{2,1,0:T(8,128)} %broadcast_in_dim.57), calls=%async_computation.5 | async-start | bytes 3670016 | tf_op jit(solution)/shard_map/all_to_all | solution.py:390
  380.2 16.2 %copy-start.1 = (f32[16,112,256]{2,1,0:T(8,128)}, f32[16,112,256]{2,1,0:T(8,128)S(1)}, u32[]{:S(2)}) copy-start(f32[16,112,256]{2,1,0:T(8,128)S(1)} %all-to-all-done.5) | copy-start | bytes 5505028
Sparse Core Ops, SparseCore 0:
  95.1 42.9 all-gather.4
  140.8 65.4 all-gather.6
